TPU v7x, 1024 devices: a whole 8x8x8 slice. The times are simulated.
1024 devices in a mesh: dp: 64 (over x_hi, z, core), group: 16 (over x_lo, y).
Axes of the slice: x: 8 (x_hi: 4, x_lo: 2; x = x_hi * 2 + x_lo), y: 8, z: 8, core: 2. Of those that a mesh axis runs over, the one named last changes fastest.
Arguments:
- layer_input: bfloat16 [16384, 8192], P('dp', 'group'), may hold values from -30 to 30
- kv_cotangent: bfloat16 [16384, 2048], P('dp', 'group'), may hold values from -70 to 70
- weight_codes: bfloat16 [2048, 8192], P('dp', 'group'), may hold values from -256 to 256
- block_scales: bfloat16 [2048, 32], P('dp', 'group'), may hold values from 0.00024986267 to 0.0009994507
- master: float32 [2048, 8192], P('dp', 'group'), may hold values from -6 to 6
- moment_one: float32 [2048, 8192], P('dp', 'group'), may hold values from -0.75 to 0.75
- moment_two: float32 [2048, 8192], P('dp', 'group'), may hold values from 0.001 to 0.01
Outputs:
- grad_input: bfloat16 [16384, 8192], P('dp', 'group')
- new_master: float32 [2048, 8192], P('dp', 'group')
- new_moment_one: float32 [2048, 8192], P('dp', 'group')
- new_moment_two: float32 [2048, 8192], P('dp', 'group')
All inputs are finite; a program needn't handle non-finite values.
Results may differ from a plain program's by a relative error of at most 0.0049.
Values may be sent and summed in bfloat16 or wider, within the bound.
No kernel may reach another device: no remote copies, remote signals or barrier semaphores. Data moves between devices by JAX's collectives and lax.ppermute only.
A program may use at most 32 MiB of HBM per device.

v0:
```python
import jax
import jax.numpy as jnp
from jax import lax
from jax.sharding import PartitionSpec as P

BLOCK = 256
CLIP = 2048


BETA_ONE = 0.9
BETA_TWO = 0.95
LEARN_RATE = 0.25
DECAY_RATE = 0.1
EPS_ADAM = 1e-08
EPS_NORM = 1e-06


def dequantize(codes, scales):
    row_count, col_count = codes.shape
    blocked = (
        codes.astype(jnp.float32).reshape(row_count, col_count // BLOCK, BLOCK)
        * scales.astype(jnp.float32)[:, :, None]
    )
    return blocked.reshape(row_count, col_count).astype(jnp.bfloat16)


def shards(layer_input, kv_cotangent, weight_codes, block_scales, master, moment_one, moment_two):
    cot_whole = lax.all_gather(kv_cotangent, "group", axis=1, tiled=True)
    codes_all = lax.all_gather(weight_codes, "dp", axis=0, tiled=True)
    scales_all = lax.all_gather(block_scales, "dp", axis=0, tiled=True)
    running = jnp.dot(
        cot_whole, dequantize(codes_all, scales_all), preferred_element_type=jnp.float32
    )
    grad_input = running.astype(jnp.bfloat16)
    partial_value = jnp.einsum(
        "tc,td->cd", cot_whole, layer_input, preferred_element_type=jnp.float32
    )
    gradient = lax.psum_scatter(
        lax.optimization_barrier(partial_value.astype(jnp.bfloat16)).astype(jnp.float32),
        "dp",
        scatter_dimension=0,
        tiled=True,
    )
    square_total = lax.psum(jnp.sum(gradient * gradient), ("dp", "group"))
    factor = jnp.minimum(1.0, CLIP / (jnp.sqrt(square_total) + EPS_NORM))
    clipped = gradient * factor
    new_moment_one = BETA_ONE * moment_one + (1.0 - BETA_ONE) * clipped
    new_moment_two = BETA_TWO * moment_two + (1.0 - BETA_TWO) * clipped * clipped
    first_fix = 1.0 - BETA_ONE**10
    second_fix = 1.0 - BETA_TWO**10
    update = new_moment_one / first_fix / (jnp.sqrt(new_moment_two / second_fix) + EPS_ADAM)
    new_master = master - LEARN_RATE * (update + DECAY_RATE * master)
    return (grad_input, new_master, new_moment_one, new_moment_two)


def solution(mesh):
    return jax.shard_map(
        shards,
        mesh=mesh,
        in_specs=(
            P("dp", "group"),
            P("dp", "group"),
            P("dp", "group"),
            P("dp", "group"),
            P("dp", "group"),
            P("dp", "group"),
            P("dp", "group"),
        ),
        out_specs=(P("dp", "group"), P("dp", "group"), P("dp", "group"), P("dp", "group")),
        check_vma=False,
    )
```

profile of v0, /device:TPU:1, one launch (start us, length us, event | category | flops | bytes accessed | tf_op | source)
XLA Modules:
  0.0 479.3 jit_solution(6447788639319741858)
XLA Ops:
  7.2 0.0 copy-start
  7.2 0.0 all-gather.6.cloned.1.call-start
  7.2 0.7 all-gather.6.cloned.1.call-update
  7.9 0.0 all-gather.4.cloned.1.call-start
  8.0 0.7 all-gather.4.cloned.1.call-update
  8.7 0.0 reduce-scatter.2.cloned.1.call-start
  8.7 72.0 %all-gather.6.cloned.1.call-done = bf16[256,2048]{1,0:T(8,128)(2,1)} async-done(((bf16[256,128]{1,0:T(8,128)(2,1)}), bf16[256,2048]{1,0:T(8,128)(2,1)}) %all-gather.6.cloned.1.call-update) | async-done | bytes 1048592 | tf_op jit(solution)/shard_map/all_gather | solution.py:28
  80.7 0.0 copy-done
  80.7 2.0 convolution_convert_fusion
  82.7 0.0 copy-start.5
  82.7 2.5 convert_element_type.27
  85.2 0.0 reduce-scatter.2.cloned.1.call-update
  85.2 0.0 copy-done.5
  85.2 96.6 %all-gather = bf16[64,32,2]{1,2,0:T(2,128)(2,1)S(1)} all-gather(bf16[1,32,2]{1,2,0:T(2,128)(2,1)S(1)} %bitcast.12), channel_id=1, replica_groups=mesh['dp'=64,'group'=16] {'dp'}, dimensions={0}, use_global_device_ids=true | all-gather | bytes 8320 | tf_op jit(solution)/shard_map/all_gather | solution.py:30
  181.8 0.1 copy.18
  181.9 0.9 copy.22
  182.9 2.5 mul.53
  185.3 0.0 copy-start.1
  185.3 2.4 copy.24
  187.8 0.8 all-gather.4.cloned.1.call-done
  188.6 0.0 copy-done.1
  188.6 0.0 copy-start.2
  188.6 0.0 copy-start.4
  188.6 3.9 fusion.2
  192.5 159.3 %reduce-scatter.2.cloned.1.call-done = f32[32,512]{1,0:T(8,128)} async-done(((f32[2048,512]{1,0:T(8,128)}), f32[32,512]{1,0:T(8,128)}) %reduce-scatter.2.cloned.1.call-update) | async-done | bytes 65552 | tf_op jit(solution)/shard_map/reduce_scatter | solution.py:38
  351.8 1.5 multiply_reduce_fusion
  353.3 0.8 copy.21
  354.1 116.3 %psum.7 = f32[]{:T(128)} all-reduce(f32[]{:T(128)} %multiply_reduce_fusion), channel_id=1, replica_groups=mesh['dp'=64,'group'=16] {'dp','group'}, use_global_device_ids=true, to_apply=%region_2.0 | all-reduce | flops 1 | bytes 8 | tf_op jit(solution)/shard_map/psum | solution.py:44
  471.2 0.0 copy-done.2
  471.2 0.0 copy-done.3
  471.2 0.0 copy-done.4
  471.2 1.5 multiply_subtract_fusion
  (1 shorter events, 0.0 us)
Async XLA Ops:
  7.2 73.5 %copy-start = (bf16[256,512]{1,0:T(8,128)(2,1)S(1)}, bf16[256,512]{1,0:T(8,128)(2,1)}, u32[]{:S(2)}) copy-start(bf16[256,512]{1,0:T(8,128)(2,1)} %param.7) | copy-start | bytes 786436
  7.2 73.5 %all-gather.6.cloned.1.call-start = ((), (), s32[]{:S(2)}) async-start(), calls=%async_computation.2 | async-start | bytes 1114112 | tf_op jit(solution)/shard_map/all_gather | solution.py:28
  7.9 180.7 %all-gather.4.cloned.1.call-start = ((), (), s32[]{:S(2)}) async-start(), calls=%async_computation.1 | async-start | bytes 2129920 | tf_op jit(solution)/shard_map/all_gather | solution.py:29
  8.7 343.2 %reduce-scatter.2.cloned.1.call-start = ((), (), s32[]{:S(2)}) async-start(), calls=%async_computation.3 | async-start | bytes 4259840 | tf_op jit(solution)/shard_map/reduce_scatter | solution.py:38
  82.7 2.6 copy-start.5
  185.3 3.3 copy-start.1
  188.6 282.6 %copy-start.2 = (f32[32,512]{1,0:T(8,128)S(1)}, f32[32,512]{1,0:T(8,128)}, u32[]{:S(2)}) copy-start(f32[32,512]{1,0:T(8,128)} %param.11) | copy-start | bytes 196612
  188.6 282.6 %copy-start.3 = (f32[32,512]{1,0:T(8,128)S(1)}, f32[32,512]{1,0:T(8,128)}, u32[]{:S(2)}) copy-start(f32[32,512]{1,0:T(8,128)} %param.12) | copy-start | bytes 196612
  188.6 282.6 %copy-start.4 = (f32[32,512]{1,0:T(8,128)S(1)}, f32[32,512]{1,0:T(8,128)}, u32[]{:S(2)}) copy-start(f32[32,512]{1,0:T(8,128)} %param.13) | copy-start | bytes 196612
Sparse Core Ops, SparseCore 0:
  10.6 70.0 all-gather.5
  85.2 103.3 all-gather.3
  194.5 157.3 reduce-scatter.1
where the time goes:
time: 480 us; the launch traced here: 479 us
  waiting for transfers between devices  233 us (49%)
  blocking collectives  213 us (44%)
  between operations  14.6 us (3%)
  local copies, waits for them, and re-layouts  6.77 us (1%)
  matrix products  5.89 us (1%)
  other arithmetic  5.53 us (1%)
    reduce_scatter x1, waiting for transfers between devices, shards(): lax.psum_scatter(lax.optimization_barrier(partial_value.astype(jnp.bfloat...  159 us
    psum x1, blocking collectives, shards(): square_total = lax.psum(jnp.sum(gradient * gradient), ('dp', 'group'))  116 us
    all_gather x1, blocking collectives, shards(): scales_all = lax.all_gather(block_scales, 'dp', axis=0, tiled=True)  96.6 us
    all_gather x1, waiting for transfers between devices, shards(): cot_whole = lax.all_gather(kv_cotangent, 'group', axis=1, tiled=True)  72 us
  transfers between devices with their start and end apart: 3, of which 3 were waited for; matrix products, arithmetic and copies ran while one was open for 3% of the time, Pallas kernels for 0%

commit v1 on v0

v1 whole, which is shorter than its diff:
```python
import jax
import jax.numpy as jnp
from jax import lax
from jax.sharding import Mesh
from jax.sharding import PartitionSpec as P

BLOCK = 256
CLIP = 2048


BETA_ONE = 0.9
BETA_TWO = 0.95
LEARN_RATE = 0.25
DECAY_RATE = 0.1
EPS_ADAM = 1e-08
EPS_NORM = 1e-06

SIZES = {"xh": 4, "z": 8, "core": 2, "xl": 2, "y": 8}
DP = ("xh", "z", "core")
GROUP = ("xl", "y")
CHIPS = ("xh", "z")
N_CHIPS = 32
N_GROUP = 16


def dequantize(codes, scales):
    row_count, col_count = codes.shape
    blocked = (
        codes.astype(jnp.float32).reshape(row_count, col_count // BLOCK, BLOCK)
        * scales.astype(jnp.float32)[:, :, None]
    )
    return blocked.reshape(row_count, col_count).astype(jnp.bfloat16)


def spread(block, axes, count):
    return lax.all_to_all(jnp.broadcast_to(block[None], (count, *block.shape)), axes, 0, 0)


def swap_cores(block):
    return lax.ppermute(block, "core", [(0, 1), (1, 0)])


def total(value, axes, count):
    return jnp.sum(spread(value, axes, count), axis=0)


def shards(layer_input, kv_cotangent, weight_codes, block_scales, master, moment_one, moment_two):
    core = lax.axis_index("core")
    rows, cols = weight_codes.shape

    weight_mine = spread(dequantize(weight_codes, block_scales), CHIPS, N_CHIPS)
    weight_other = swap_cores(weight_mine)
    weight = jnp.where(
        core == 0,
        jnp.stack([weight_mine, weight_other], axis=1),
        jnp.stack([weight_other, weight_mine], axis=1),
    ).reshape(N_CHIPS * 2 * rows, cols)

    cot = spread(kv_cotangent, GROUP, N_GROUP)
    cot_whole = cot.transpose(1, 0, 2).reshape(kv_cotangent.shape[0], -1)
    partial_value = jnp.einsum(
        "tc,td->cd", cot_whole, layer_input, preferred_element_type=jnp.float32
    ).astype(jnp.bfloat16)
    halves = partial_value.reshape(N_CHIPS, 2, rows, cols)
    keep = lax.dynamic_index_in_dim(halves, core, 1, keepdims=False)
    give = lax.dynamic_index_in_dim(halves, 1 - core, 1, keepdims=False)
    pair = keep.astype(jnp.float32) + swap_cores(give).astype(jnp.float32)
    pieces = lax.all_to_all(pair.astype(jnp.bfloat16), CHIPS, 0, 0)
    gradient = jnp.sum(pieces.astype(jnp.float32), axis=0)

    squares = jnp.sum((gradient * gradient).reshape(-1, 8, 128), axis=0)
    square_total = jnp.sum(total(total(squares, DP, 64), GROUP, N_GROUP))
    factor = jnp.minimum(1.0, CLIP / (jnp.sqrt(square_total) + EPS_NORM))
    clipped = gradient * factor
    new_moment_one = BETA_ONE * moment_one + (1.0 - BETA_ONE) * clipped
    new_moment_two = BETA_TWO * moment_two + (1.0 - BETA_TWO) * clipped * clipped
    first_fix = 1.0 - BETA_ONE**10
    second_fix = 1.0 - BETA_TWO**10
    update = new_moment_one / first_fix / (jnp.sqrt(new_moment_two / second_fix) + EPS_ADAM)
    new_master = master - LEARN_RATE * (update + DECAY_RATE * master)

    grad_input = jnp.dot(cot_whole, weight, preferred_element_type=jnp.float32).astype(jnp.bfloat16)
    return (grad_input, new_master, new_moment_one, new_moment_two)


def solution(mesh):
    fine = Mesh(mesh.devices.reshape(tuple(SIZES.values())), tuple(SIZES))
    return jax.shard_map(
        shards,
        mesh=fine,
        in_specs=(P(DP, GROUP),) * 7,
        out_specs=(P(DP, GROUP),) * 4,
        check_vma=False,
    )
```

time: 480 us -> 176 us (0.37)
  blocking collectives: 213 us -> 0 us
  waiting for transfers between devices: 233 us -> 85.1 us
  starting transfers between devices: 0.11 us -> 69.2 us
  between operations: 14.6 us -> 1.55 us
    reduce_scatter x1 -> x0, waiting for transfers between devices: 159 us -> none  [shards(): lax.psum_scatter(lax.optimization_barrier(partial_value.astype(jnp.bfloat...]
    psum x1 -> x0, blocking collectives: 116 us -> none  [shards(): square_total = lax.psum(jnp.sum(gradient * gradient), ('dp', 'group'))]
    all_gather x1 -> x0, blocking collectives: 96.6 us -> none  [shards(): scales_all = lax.all_gather(block_scales, 'dp', axis=0, tiled=True)]
    all_to_all x0 -> x5, waiting for transfers between devices: none -> 82.5 us  [the longest x4 55.2 us: spread(): lax.all_to_all(jnp.broadcast_to(block[None], (count, *block.shape)), axes...]
    all_gather x2 -> x0, waiting for transfers between devices: 72.8 us -> none  [the longest x1 72 us: shards(): cot_whole = lax.all_gather(kv_cotangent, 'group', axis=1, tiled=True)]
    all_to_all x0 -> x5, starting transfers between devices: none -> 62.7 us  [the longest x4 51.3 us: spread(): lax.all_to_all(jnp.broadcast_to(block[None], (count, *block.shape)), axes...]
    ppermute x0 -> x2, starting transfers between devices: none -> 6.47 us  [swap_cores(): return lax.ppermute(block, 'core', [(0, 1), (1, 0)])]
  transfers between devices with their start and end apart: 3 -> 7, of which waited for: 3 -> 6; matrix products, arithmetic and copies ran while one was open for 3% -> 6% of each run, Pallas kernels for 0% -> 0%
where the time goes in v1:
time: 176 us; the launch traced here: 175 us
  waiting for transfers between devices  85.1 us (48%)
  starting transfers between devices  69.2 us (39%)
  other arithmetic  8.65 us (5%)
  local copies, waits for them, and re-layouts  8.64 us (5%)
  matrix products  2.16 us (1%)
    all_to_all x4, waiting for transfers between devices, spread(): lax.all_to_all(jnp.broadcast_to(block[None], (count, *block.shape)), axes...  55.2 us
    all_to_all x4, starting transfers between devices, spread(): lax.all_to_all(jnp.broadcast_to(block[None], (count, *block.shape)), axes...  51.3 us
    all_to_all x1, waiting for transfers between devices, shards(): pieces = lax.all_to_all(pair.astype(jnp.bfloat16), CHIPS, 0, 0)  27.4 us
    all_to_all x1, starting transfers between devices, shards(): pieces = lax.all_to_all(pair.astype(jnp.bfloat16), CHIPS, 0, 0)  11.4 us
    ppermute x2, starting transfers between devices, swap_cores(): return lax.ppermute(block, 'core', [(0, 1), (1, 0)])  6.47 us
    unnamed x11, local copies, waits for them, and re-layouts  3.81 us
    broadcast_in_dim x4, local copies, waits for them, and re-layouts, spread(): jnp.broadcast_to(block[None], (count, *block.shape))  3.58 us
  transfers between devices with their start and end apart: 7, of which 6 were waited for; matrix products, arithmetic and copies ran while one was open for 6% of the time, Pallas kernels for 0%

profile of v1, /device:TPU:1, one launch (start us, length us, event | category | flops | bytes accessed | tf_op | source)
XLA Modules:
  0.0 175.4 jit_solution(10579631328647096359)
XLA Ops:
  0.6 0.0 copy-start
  0.7 1.0 copy.17
  1.6 1.1 broadcast_in_dim.9
  2.7 9.1 %all-to-all-start.1 = ((bf16[16,256,128]{1,2,0:T(8,128)(2,1)}), bf16[16,256,128]{1,2,0:T(8,128)(2,1)S(1)}, u32[]{:S(2)}, u32[]{:S(2)}) async-start(bf16[16,256,128]{1,2,0:T(8,128)(2,1)} %broadcast_in_dim.9), calls=%async_computation.1 | async-start | bytes 2097152 | tf_op jit(solution)/shard_map/all_to_all | solution.py:36
  11.9 0.1 copy.16
  12.0 0.1 mul.57
  12.1 22.8 %all-to-all-done.1 = bf16[16,256,128]{1,2,0:T(8,128)(2,1)S(1)} async-done(((bf16[16,256,128]{1,2,0:T(8,128)(2,1)}), bf16[16,256,128]{1,2,0:T(8,128)(2,1)S(1)}, u32[]{:S(2)}, u32[]{:S(2)}) %all-to-all-start.1) | async-done | bytes 1048608 | tf_op jit(solution)/shard_map/all_to_all | solution.py:36
  34.9 1.1 broadcast_in_dim.8
  36.1 23.3 %all-to-all-start = ((bf16[32,32,512]{2,1,0:T(8,128)(2,1)}), bf16[32,32,512]{2,1,0:T(8,128)(2,1)}, u32[]{:S(2)}, u32[]{:S(2)}) async-start(bf16[32,32,512]{2,1,0:T(8,128)(2,1)} %broadcast_in_dim.8), calls=%async_computation | async-start | bytes 2097152 | tf_op jit(solution)/shard_map/all_to_all | solution.py:36
  59.3 0.7 convolution_convert_fusion
  60.1 1.1 dynamic-slice_bitcast_fusion
  61.1 3.6 %collective-permute-start.1 = (bf16[32,32,512]{2,1,0:T(8,128)(2,1)}, bf16[32,32,512]{2,1,0:T(8,128)(2,1)}, u32[]{:S(2)}, u32[]{:S(2)}) collective-permute-start(bf16[32,32,512]{2,1,0:T(8,128)(2,1)} %dynamic-slice_bitcast_fusion), channel_id=1, source_target_pairs={{0,16},{16,0},{1,17},{17,1},{2,18},{18,2},{3,19},{19,3},{4,20},{20... | collective-permute-start | bytes 3145736 | tf_op jit(solution)/shard_map/ppermute | solution.py:40
  64.7 2.6 %collective-permute-done.1 = bf16[32,32,512]{2,1,0:T(8,128)(2,1)} collective-permute-done((bf16[32,32,512]{2,1,0:T(8,128)(2,1)}, bf16[32,32,512]{2,1,0:T(8,128)(2,1)}, u32[]{:S(2)}, u32[]{:S(2)}) %collective-permute-start.1) | collective-permute-done | bytes 1048608 | tf_op jit(solution)/shard_map/ppermute | solution.py:40
  67.3 2.6 %fusion = bf16[32,32,512]{2,1,0:T(8,128)(2,1)} fusion(bf16[32,32,512]{2,1,0:T(8,128)(2,1)} %collective-permute-done.1, bf16[32,2,32,512]{3,2,1,0:T(8,128)(2,1)S(1)} %bitcast.24, s32[]{:T(128)S(6)} %select_n.28), kind=kLoop, calls=%fused_computation.3 | loop fusion | flops 2097152 | bytes 3145732 | tf_op jit(solution)/shard_map/convert_element_type | solution.py:68
  69.9 17.9 %all-to-all-done = bf16[32,32,512]{2,1,0:T(8,128)(2,1)} async-done(((bf16[32,32,512]{2,1,0:T(8,128)(2,1)}), bf16[32,32,512]{2,1,0:T(8,128)(2,1)}, u32[]{:S(2)}, u32[]{:S(2)}) %all-to-all-start) | async-done | bytes 1048608 | tf_op jit(solution)/shard_map/all_to_all | solution.py:36
  87.7 11.4 %all-to-all-start.2 = ((bf16[32,32,512]{2,1,0:T(8,128)(2,1)}), bf16[32,32,512]{2,1,0:T(8,128)(2,1)S(1)}, u32[]{:S(2)}, u32[]{:S(2)}) async-start(bf16[32,32,512]{2,1,0:T(8,128)(2,1)} %fusion), calls=%async_computation.2 | async-start | bytes 2097152 | tf_op jit(solution)/shard_map/all_to_all | solution.py:68
  99.2 2.9 %collective-permute-start = (bf16[32,32,512]{2,1,0:T(8,128)(2,1)}, bf16[32,32,512]{2,1,0:T(8,128)(2,1)S(1)}, u32[]{:S(2)}, u32[]{:S(2)}) collective-permute-start(bf16[32,32,512]{2,1,0:T(8,128)(2,1)} %all-to-all-done), channel_id=1, source_target_pairs={{0,16},{16,0},{1,17},{17,1},{2,18},{18,2},{3,19},{19,3},{4,20},{20... | collective-permute-start | bytes 3145736 | tf_op jit(solution)/shard_map/ppermute | solution.py:40
  102.1 27.4 %all-to-all-done.2 = bf16[32,32,512]{2,1,0:T(8,128)(2,1)S(1)} async-done(((bf16[32,32,512]{2,1,0:T(8,128)(2,1)}), bf16[32,32,512]{2,1,0:T(8,128)(2,1)S(1)}, u32[]{:S(2)}, u32[]{:S(2)}) %all-to-all-start.2) | async-done | bytes 1048608 | tf_op jit(solution)/shard_map/all_to_all | solution.py:68
  129.4 0.2 convert_reduce_fusion
  129.6 0.7 broadcast_in_dim.10
  130.3 8.7 %all-to-all-start.3 = ((f32[64,8,128]{2,1,0:T(8,128)}), f32[64,8,128]{2,1,0:T(8,128)}, u32[]{:S(2)}, u32[]{:S(2)}) async-start(f32[64,8,128]{2,1,0:T(8,128)} %broadcast_in_dim.10), calls=%async_computation.3 | async-start | bytes 524288 | tf_op jit(solution)/shard_map/all_to_all | solution.py:36
  139.1 1.0 copy-done.1
  140.1 2.6 %maximum_select_fusion = bf16[32,2,32,512]{3,2,1,0:T(8,128)(2,1)S(1)} fusion(bf16[32,1,32,512]{3,2,1,0:T(8,128)(2,1)} %bitcast.25, bf16[32,1,32,512]{3,2,1,0:T(8,128)(2,1)} %bitcast, pred[]{:T(512)S(6)} %eq.3), kind=kLoop, calls=%fused_computation.1 | loop fusion | flops 3145728 | bytes 4194305 | tf_op jit(solution)/shard_map/jit(_where)/select_n | solution.py:53
  142.7 10.4 %all-to-all-done.3 = f32[64,8,128]{2,1,0:T(8,128)} async-done(((f32[64,8,128]{2,1,0:T(8,128)}), f32[64,8,128]{2,1,0:T(8,128)}, u32[]{:S(2)}, u32[]{:S(2)}) %all-to-all-start.3) | async-done | bytes 262176 | tf_op jit(solution)/shard_map/all_to_all | solution.py:36
  153.1 1.0 reduce_sum.42
  154.1 0.6 broadcast_in_dim.11
  154.8 10.3 %all-to-all-start.4 = ((f32[16,8,128]{2,1,0:T(8,128)}), f32[16,8,128]{2,1,0:T(8,128)S(1)}, u32[]{:S(2)}, u32[]{:S(2)}) async-start(f32[16,8,128]{2,1,0:T(8,128)} %broadcast_in_dim.11), calls=%async_computation.4 | async-start | bytes 131072 | tf_op jit(solution)/shard_map/all_to_all | solution.py:36
  165.0 1.5 fusion.1
  166.5 1.8 %copy.18 = bf16[256,512]{1,0:T(8,128)(2,1)} copy(bf16[256,512]{0,1:T(8,128)(2,1)} %fusion.1) | data formatting | bytes 524288
  168.3 4.1 %all-to-all-done.4 = f32[16,8,128]{2,1,0:T(8,128)S(1)} async-done(((f32[16,8,128]{2,1,0:T(8,128)}), f32[16,8,128]{2,1,0:T(8,128)S(1)}, u32[]{:S(2)}, u32[]{:S(2)}) %all-to-all-start.4) | async-done | bytes 65568 | tf_op jit(solution)/shard_map/all_to_all | solution.py:36
  172.4 0.6 reduce_sum.43
  173.7 1.6 multiply_subtract_fusion
  (12 shorter events, 0.1 us)
Async XLA Ops:
  0.6 58.7 %copy-start = (bf16[256,512]{1,0:T(8,128)(2,1)S(1)}, bf16[256,512]{1,0:T(8,128)(2,1)}, u32[]{:S(2)}) copy-start(bf16[256,512]{1,0:T(8,128)(2,1)} %param.7) | copy-start | bytes 786436
  0.6 11.2 %copy-start.3 = (bf16[32,2]{0,1:T(2,128)(2,1)S(1)}, bf16[32,2]{0,1:T(2,128)(2,1)}, u32[]{:S(2)}) copy-start(bf16[32,2]{0,1:T(2,128)(2,1)} %param.10) | copy-start | bytes 388
  0.7 11.4 %copy-start.2 = (bf16[32,512]{1,0:T(8,128)(2,1)S(1)}, bf16[32,512]{1,0:T(8,128)(2,1)}, u32[]{:S(2)}) copy-start(bf16[32,512]{1,0:T(8,128)(2,1)} %param.9) | copy-start | bytes 98308
  2.7 32.2 %all-to-all-start.1 = ((bf16[16,256,128]{1,2,0:T(8,128)(2,1)}), bf16[16,256,128]{1,2,0:T(8,128)(2,1)S(1)}, u32[]{:S(2)}, u32[]{:S(2)}) async-start(bf16[16,256,128]{1,2,0:T(8,128)(2,1)} %broadcast_in_dim.9), calls=%async_computation.1 | async-start | bytes 2097152 | tf_op jit(solution)/shard_map/all_to_all | solution.py:36
  36.1 51.7 %all-to-all-start = ((bf16[32,32,512]{2,1,0:T(8,128)(2,1)}), bf16[32,32,512]{2,1,0:T(8,128)(2,1)}, u32[]{:S(2)}, u32[]{:S(2)}) async-start(bf16[32,32,512]{2,1,0:T(8,128)(2,1)} %broadcast_in_dim.8), calls=%async_computation | async-start | bytes 2097152 | tf_op jit(solution)/shard_map/all_to_all | solution.py:36
  61.1 6.2 %collective-permute-start.1 = (bf16[32,32,512]{2,1,0:T(8,128)(2,1)}, bf16[32,32,512]{2,1,0:T(8,128)(2,1)}, u32[]{:S(2)}, u32[]{:S(2)}) collective-permute-start(bf16[32,32,512]{2,1,0:T(8,128)(2,1)} %dynamic-slice_bitcast_fusion), channel_id=1, source_target_pairs={{0,16},{16,0},{1,17},{17,1},{2,18},{18,2},{3,19},{19,3},{4,20},{20... | collective-permute-start | bytes 3145736 | tf_op jit(solution)/shard_map/ppermute | solution.py:40
  87.7 41.7 %all-to-all-start.2 = ((bf16[32,32,512]{2,1,0:T(8,128)(2,1)}), bf16[32,32,512]{2,1,0:T(8,128)(2,1)S(1)}, u32[]{:S(2)}, u32[]{:S(2)}) async-start(bf16[32,32,512]{2,1,0:T(8,128)(2,1)} %fusion), calls=%async_computation.2 | async-start | bytes 2097152 | tf_op jit(solution)/shard_map/all_to_all | solution.py:68
  99.2 39.9 %collective-permute-start = (bf16[32,32,512]{2,1,0:T(8,128)(2,1)}, bf16[32,32,512]{2,1,0:T(8,128)(2,1)S(1)}, u32[]{:S(2)}, u32[]{:S(2)}) collective-permute-start(bf16[32,32,512]{2,1,0:T(8,128)(2,1)} %all-to-all-done), channel_id=1, source_target_pairs={{0,16},{16,0},{1,17},{17,1},{2,18},{18,2},{3,19},{19,3},{4,20},{20... | collective-permute-start | bytes 3145736 | tf_op jit(solution)/shard_map/ppermute | solution.py:40
  130.3 22.8 %all-to-all-start.3 = ((f32[64,8,128]{2,1,0:T(8,128)}), f32[64,8,128]{2,1,0:T(8,128)}, u32[]{:S(2)}, u32[]{:S(2)}) async-start(f32[64,8,128]{2,1,0:T(8,128)} %broadcast_in_dim.10), calls=%async_computation.3 | async-start | bytes 524288 | tf_op jit(solution)/shard_map/all_to_all | solution.py:36
  139.0 1.0 copy-start.1
  154.8 17.6 %all-to-all-start.4 = ((f32[16,8,128]{2,1,0:T(8,128)}), f32[16,8,128]{2,1,0:T(8,128)S(1)}, u32[]{:S(2)}, u32[]{:S(2)}) async-start(f32[16,8,128]{2,1,0:T(8,128)} %broadcast_in_dim.11), calls=%async_computation.4 | async-start | bytes 131072 | tf_op jit(solution)/shard_map/all_to_all | solution.py:36

commit v2 on v1

v2 whole, which is shorter than its diff:
```python
import functools

import jax
import jax.numpy as jnp
from jax import lax
from jax.experimental import pallas as pl
from jax.experimental.pallas import tpu as pltpu
from jax.sharding import Mesh
from jax.sharding import PartitionSpec as P

BLOCK = 256
CLIP = 2048


BETA_ONE = 0.9
BETA_TWO = 0.95
LEARN_RATE = 0.25
DECAY_RATE = 0.1
EPS_ADAM = 1e-08
EPS_NORM = 1e-06

SIZES = {"xh": 4, "z": 8, "core": 2, "xl": 2, "y": 8}
DP = ("xh", "z", "core")
GROUP = ("xl", "y")
CHIPS = ("xh", "z")
N_CHIPS = 32
N_GROUP = 16
N_ALL = 1024


def dequantize(codes, scales):
    row_count, col_count = codes.shape
    blocked = (
        codes.astype(jnp.float32).reshape(row_count, col_count // BLOCK, BLOCK)
        * scales.astype(jnp.float32)[:, :, None]
    )
    return blocked.reshape(row_count, col_count).astype(jnp.bfloat16)


def spread(block, axes, count):
    return lax.all_to_all(jnp.broadcast_to(block[None], (count, *block.shape)), axes, 0, 0)


def swap_cores(block):
    return lax.ppermute(block, "core", [(0, 1), (1, 0)])


def fetch(block, axis, distance):
    size = SIZES[axis]
    return lax.ppermute(block, axis, [(i, (i - distance) % size) for i in range(size)])


def collect(block, order, axis, distances):
    for d in distances:
        block = jnp.concatenate([block, fetch(block, axis, d)], axis=0)
        order = order + [(x + d, z) if axis == "xh" else (x, z + d) for x, z in order]
    return block, order


def order_rows_kernel(order, rows, place_ref, mine_ref, other_ref, out_ref):
    x_own, z_own, core = place_ref[0], place_ref[1], place_ref[2]
    for i, (dx, dz) in enumerate(order):
        chip = lax.rem(x_own + dx, SIZES["xh"]) * SIZES["z"] + lax.rem(z_own + dz, SIZES["z"])
        for source, side in ((mine_ref, core), (other_ref, 1 - core)):
            start = pl.multiple_of((chip * 2 + side) * rows, rows)
            out_ref[pl.ds(start, rows), :] = source[i * rows : (i + 1) * rows, :]


def order_rows(mine, other, order, rows):
    place = jnp.stack([lax.axis_index("xh"), lax.axis_index("z"), lax.axis_index("core")])
    size = 2 * mine.shape[0] * mine.shape[1]
    return pl.pallas_call(
        functools.partial(order_rows_kernel, order, rows),
        out_shape=jax.ShapeDtypeStruct((2 * mine.shape[0], mine.shape[1]), mine.dtype),
        in_specs=[
            pl.BlockSpec(memory_space=pltpu.SMEM),
            pl.BlockSpec(memory_space=pltpu.VMEM),
            pl.BlockSpec(memory_space=pltpu.VMEM),
        ],
        out_specs=pl.BlockSpec(memory_space=pltpu.VMEM),
        cost_estimate=pl.CostEstimate(flops=0, bytes_accessed=4 * size, transcendentals=0),
        compiler_params=pltpu.CompilerParams(vmem_limit_bytes=8 * 2**20),
        name="order_rows",
    )(place.astype(jnp.int32), mine, other)


def shards(layer_input, kv_cotangent, weight_codes, block_scales, master, moment_one, moment_two):
    core = lax.axis_index("core")
    rows, cols = weight_codes.shape
    tokens = kv_cotangent.shape[0]

    cot = spread(kv_cotangent.T, GROUP, N_GROUP).reshape(-1, tokens)
    input_other = swap_cores(layer_input)
    mine, order = collect(dequantize(weight_codes, block_scales), [(0, 0)], "xh", (2, 1))
    mine, order = collect(mine, order, "z", (4,))
    cot, input_other, mine = lax.optimization_barrier((cot, input_other, mine))
    halves = cot.reshape(N_CHIPS, 2, rows, tokens)
    keep = lax.dynamic_index_in_dim(halves, core, 1, keepdims=False)
    cot_other = swap_cores(lax.dynamic_index_in_dim(halves, 1 - core, 1, keepdims=False))
    pair = jnp.einsum("crt,td->crd", keep, layer_input, preferred_element_type=jnp.float32)
    pair += jnp.einsum("crt,td->crd", cot_other, input_other, preferred_element_type=jnp.float32)
    pieces = lax.all_to_all(pair.astype(jnp.bfloat16), CHIPS, 0, 0)
    mine, order = collect(mine, order, "z", (2, 1))
    pieces, mine = lax.optimization_barrier((pieces, mine))
    gradient = jnp.sum(pieces.astype(jnp.float32), axis=0)

    squares = jnp.sum(gradient * gradient, axis=0, keepdims=True)
    squares = sum(squares[:, i : i + 128] for i in range(0, cols, 128))
    squares = spread(squares, DP + GROUP, N_ALL)

    weight = order_rows(mine, swap_cores(mine), order, rows)
    grad_input = jnp.einsum(
        "ct,cd->td", cot, weight, preferred_element_type=jnp.float32
    ).astype(jnp.bfloat16)
    squares, grad_input = lax.optimization_barrier((squares, grad_input))

    square_total = jnp.sum(squares)
    factor = jnp.minimum(1.0, CLIP / (jnp.sqrt(square_total) + EPS_NORM))
    clipped = gradient * factor
    new_moment_one = BETA_ONE * moment_one + (1.0 - BETA_ONE) * clipped
    new_moment_two = BETA_TWO * moment_two + (1.0 - BETA_TWO) * clipped * clipped
    first_fix = 1.0 - BETA_ONE**10
    second_fix = 1.0 - BETA_TWO**10
    update = new_moment_one / first_fix / (jnp.sqrt(new_moment_two / second_fix) + EPS_ADAM)
    new_master = master - LEARN_RATE * (update + DECAY_RATE * master)

    return (grad_input, new_master, new_moment_one, new_moment_two)


def solution(mesh):
    fine = Mesh(mesh.devices.reshape(tuple(SIZES.values())), tuple(SIZES))
    return jax.shard_map(
        shards,
        mesh=fine,
        in_specs=(P(DP, GROUP),) * 7,
        out_specs=(P(DP, GROUP),) * 4,
        check_vma=False,
    )
```

time: 176 us -> 183 us (1.040)
  starting transfers between devices: 69.2 us -> 93.1 us
  waiting for transfers between devices: 85.1 us -> 76.6 us
  local copies, waits for them, and re-layouts: 8.64 us -> 3.4 us
  other arithmetic: 8.65 us -> 3.84 us
    ppermute x0 -> x5, waiting for transfers between devices: none -> 56.7 us  [fetch(): lax.ppermute(block, axis, [(i, (i - distance) % size) for i in range(size)])]
    all_to_all x4 -> x2, waiting for transfers between devices: 55.2 us -> 18.8 us  [spread(): lax.all_to_all(jnp.broadcast_to(block[None], (count, *block.shape)), axes...]
    ppermute x0 -> x5, starting transfers between devices: none -> 31.1 us  [fetch(): lax.ppermute(block, axis, [(i, (i - distance) % size) for i in range(size)])]
    all_to_all x1, waiting for transfers between devices: 27.4 us -> 0.01 us  [shards(): pieces = lax.all_to_all(pair.astype(jnp.bfloat16), CHIPS, 0, 0)]
    all_to_all x4 -> x2, starting transfers between devices: 51.3 us -> 37 us  [spread(): lax.all_to_all(jnp.broadcast_to(block[None], (count, *block.shape)), axes...]
    ppermute x2 -> x3, starting transfers between devices: 6.47 us -> 15 us  [swap_cores(): return lax.ppermute(block, 'core', [(0, 1), (1, 0)])]
    unnamed x11 -> x13, local copies, waits for them, and re-layouts: 3.81 us -> 0.04 us
    select_n x1 -> x0, other arithmetic: 2.64 us -> none  [shards(): jnp.where(core == 0, jnp.stack([weight_mine, weight_other], axis=1), jnp....]
  transfers between devices with their start and end apart: 7 -> 11, of which waited for: 6 -> 6; matrix products, arithmetic and copies ran while one was open for 6% -> 2% of each run, Pallas kernels for 0% -> 0%
where the time goes in v2:
time: 183 us
  starting transfers between devices  93.1 us (51%)
  waiting for transfers between devices  76.6 us (42%)
  other arithmetic  3.84 us (2%)
  local copies, waits for them, and re-layouts  3.4 us (2%)
  matrix products  3.27 us (2%)
    ppermute x5, waiting for transfers between devices, fetch(): lax.ppermute(block, axis, [(i, (i - distance) % size) for i in range(size)])  56.7 us
    all_to_all x2, starting transfers between devices, spread(): lax.all_to_all(jnp.broadcast_to(block[None], (count, *block.shape)), axes...  37 us
    ppermute x5, starting transfers between devices, fetch(): lax.ppermute(block, axis, [(i, (i - distance) % size) for i in range(size)])  31.1 us
    all_to_all x2, waiting for transfers between devices, spread(): lax.all_to_all(jnp.broadcast_to(block[None], (count, *block.shape)), axes...  18.8 us
    ppermute x3, starting transfers between devices, swap_cores(): return lax.ppermute(block, 'core', [(0, 1), (1, 0)])  15 us
    all_to_all x1, starting transfers between devices, shards(): pieces = lax.all_to_all(pair.astype(jnp.bfloat16), CHIPS, 0, 0)  10.1 us
  transfers between devices with their start and end apart: 11, of which 6 were waited for; matrix products, arithmetic and copies ran while one was open for 2% of the time, Pallas kernels for 0%

profile of v2, /device:TPU:1, one launch (start us, length us, event | category | flops | bytes accessed | tf_op | source)
XLA Modules:
  0.0 182.7 jit_solution(6500822826745491718)
XLA Ops:
  0.7 1.0 copy.13
  1.6 1.1 broadcast_in_dim.8
  2.7 9.1 %all-to-all-start = ((bf16[16,128,256]{2,1,0:T(8,128)(2,1)}), bf16[16,128,256]{2,1,0:T(8,128)(2,1)S(1)}, u32[]{:S(2)}, u32[]{:S(2)}) async-start(bf16[16,128,256]{2,1,0:T(8,128)(2,1)} %broadcast_in_dim.8), calls=%async_computation | async-start | bytes 2097152 | tf_op jit(solution)/shard_map/all_to_all | solution.py:41
  11.9 0.1 copy.14
  12.0 0.1 mul.53
  12.1 6.2 %collective-permute-start.1 = (bf16[32,512]{1,0:T(8,128)(2,1)S(1)}, bf16[32,512]{1,0:T(8,128)(2,1)S(1)}, u32[]{:S(2)}, u32[]{:S(2)}) collective-permute-start(bf16[32,512]{1,0:T(8,128)(2,1)S(1)} %multiply_convert_fusion), channel_id=1, source_target_pairs={{0,512},{256,768},{512,0},{768,256},{1,513},{257,769},{513,1},{769... | collective-permute-start | bytes 98312 | tf_op jit(solution)/shard_map/ppermute | solution.py:50
  18.3 11.3 %collective-permute-done.1 = bf16[32,512]{1,0:T(8,128)(2,1)S(1)} collective-permute-done((bf16[32,512]{1,0:T(8,128)(2,1)S(1)}, bf16[32,512]{1,0:T(8,128)(2,1)S(1)}, u32[]{:S(2)}, u32[]{:S(2)}) %collective-permute-start.1) | collective-permute-done | bytes 32800 | tf_op jit(solution)/shard_map/ppermute | solution.py:50
  29.6 3.2 %collective-permute-start.2 = (bf16[64,512]{1,0:T(8,128)(2,1)S(1)}, bf16[64,512]{1,0:T(8,128)(2,1)S(1)}, u32[]{:S(2)}, u32[]{:S(2)}) collective-permute-start(bf16[64,512]{1,0:T(8,128)(2,1)S(1)} %pad_maximum_fusion.4), channel_id=1, source_target_pairs={{0,768},{256,0},{512,256},{768,512},{1,769},{257,1},{513,257},{769... | collective-permute-start | bytes 196616 | tf_op jit(solution)/shard_map/ppermute | solution.py:50
  32.9 4.2 %collective-permute-start = (bf16[256,512]{1,0:T(8,128)(2,1)S(1)}, bf16[256,512]{1,0:T(8,128)(2,1)S(1)}, u32[]{:S(2)}, u32[]{:S(2)}) collective-permute-start(bf16[256,512]{1,0:T(8,128)(2,1)S(1)} %copy-done), channel_id=1, source_target_pairs={{0,16},{16,0},{1,17},{17,1},{2,18},{18,2},{3,19},{19,3},{4,20},{20... | collective-permute-start | bytes 786440 | tf_op jit(solution)/shard_map/ppermute | solution.py:45
  37.1 14.5 %collective-permute-start.3 = (bf16[128,512]{1,0:T(8,128)(2,1)S(1)}, bf16[128,512]{1,0:T(8,128)(2,1)S(1)}, u32[]{:S(2)}, u32[]{:S(2)}) collective-permute-start(bf16[128,512]{1,0:T(8,128)(2,1)S(1)} %pad_maximum_fusion.3), channel_id=1, source_target_pairs={{0,128},{32,160},{64,192},{96,224},{128,0},{160,32},{192,64},{224,... | collective-permute-start | bytes 393224 | tf_op jit(solution)/shard_map/ppermute | solution.py:50
  51.6 2.3 %collective-permute-done.3 = bf16[128,512]{1,0:T(8,128)(2,1)S(1)} collective-permute-done((bf16[128,512]{1,0:T(8,128)(2,1)S(1)}, bf16[128,512]{1,0:T(8,128)(2,1)S(1)}, u32[]{:S(2)}, u32[]{:S(2)}) %collective-permute-start.3) | collective-permute-done | bytes 131104 | tf_op jit(solution)/shard_map/ppermute | solution.py:50
  54.1 6.6 %collective-permute-start.4 = (bf16[32,32,256]{2,1,0:T(8,128)(2,1)S(1)}, bf16[32,32,256]{2,1,0:T(8,128)(2,1)S(1)}, u32[]{:S(2)}, u32[]{:S(2)}) collective-permute-start(bf16[32,32,256]{2,1,0:T(8,128)(2,1)S(1)} %dynamic-slice_bitcast_fusion), channel_id=1, source_target_pairs={{0,16},{16,0},{1,17},{17,1},{2,18},{18,2},{3,19},{19,3},{4,20},{20... | collective-permute-start | bytes 1572872 | tf_op jit(solution)/shard_map/ppermute | solution.py:45
  60.7 0.4 fusion
  61.1 1.1 collective-permute-done.4
  62.2 1.4 add_convert_fusion
  63.6 10.1 %all-to-all-start.1 = ((bf16[32,32,512]{2,1,0:T(8,128)(2,1)}), bf16[32,32,512]{2,1,0:T(8,128)(2,1)S(1)}, u32[]{:S(2)}, u32[]{:S(2)}) async-start(bf16[32,32,512]{2,1,0:T(8,128)(2,1)} %add_convert_fusion), calls=%async_computation.1 | async-start | bytes 2097152 | tf_op jit(solution)/shard_map/all_to_all | solution.py:102
  73.7 5.2 %collective-permute-start.5 = (bf16[256,512]{1,0:T(8,128)(2,1)S(1)}, bf16[256,512]{1,0:T(8,128)(2,1)S(1)}, u32[]{:S(2)}, u32[]{:S(2)}) collective-permute-start(bf16[256,512]{1,0:T(8,128)(2,1)S(1)} %pad_maximum_fusion.2), channel_id=1, source_target_pairs={{0,192},{32,224},{64,0},{96,32},{128,64},{160,96},{192,128},{224,1... | collective-permute-start | bytes 786440 | tf_op jit(solution)/shard_map/ppermute | solution.py:50
  78.9 31.0 %collective-permute-done.5 = bf16[256,512]{1,0:T(8,128)(2,1)S(1)} collective-permute-done((bf16[256,512]{1,0:T(8,128)(2,1)S(1)}, bf16[256,512]{1,0:T(8,128)(2,1)S(1)}, u32[]{:S(2)}, u32[]{:S(2)}) %collective-permute-start.5) | collective-permute-done | bytes 262176 | tf_op jit(solution)/shard_map/ppermute | solution.py:50
  110.0 1.9 %collective-permute-start.6 = (bf16[512,512]{1,0:T(8,128)(2,1)S(1)}, bf16[512,512]{1,0:T(8,128)(2,1)S(1)}, u32[]{:S(2)}, u32[]{:S(2)}) collective-permute-start(bf16[512,512]{1,0:T(8,128)(2,1)S(1)} %pad_maximum_fusion.1), channel_id=1, source_target_pairs={{0,224},{32,0},{64,32},{96,64},{128,96},{160,128},{192,160},{224,1... | collective-permute-start | bytes 1572872 | tf_op jit(solution)/shard_map/ppermute | solution.py:50
  111.9 12.1 %collective-permute-done.6 = bf16[512,512]{1,0:T(8,128)(2,1)S(1)} collective-permute-done((bf16[512,512]{1,0:T(8,128)(2,1)S(1)}, bf16[512,512]{1,0:T(8,128)(2,1)S(1)}, u32[]{:S(2)}, u32[]{:S(2)}) %collective-permute-start.6) | collective-permute-done | bytes 524320 | tf_op jit(solution)/shard_map/ppermute | solution.py:50
  124.0 0.1 pad_maximum_fusion.mine_ref
  124.1 0.2 convert_reduce_fusion
  124.2 4.2 %collective-permute-start.7 = (bf16[1024,512]{1,0:T(8,128)(2,1)S(1)}, bf16[1024,512]{1,0:T(8,128)(2,1)S(1)}, u32[]{:S(2)}, u32[]{:S(2)}) collective-permute-start(bf16[1024,512]{1,0:T(8,128)(2,1)S(1)} %pad_maximum_fusion.mine_ref), channel_id=1, source_target_pairs={{0,16},{16,0},{1,17},{17,1},{2,18},{18,2},{3,19},{19,3},{4,20},{20... | collective-permute-start | bytes 3145736 | tf_op jit(solution)/shard_map/ppermute | solution.py:45
  128.4 1.1 broadcast_in_dim.21
  129.5 27.9 %all-to-all-start.2 = ((f32[1024,1,128]{2,1,0:T(1,128)}), f32[1024,1,128]{2,1,0:T(1,128)}, u32[]{:S(2)}, u32[]{:S(2)}) async-start(f32[1024,1,128]{2,1,0:T(1,128)} %broadcast_in_dim.21), calls=%async_computation.2 | async-start | bytes 1048576 | tf_op jit(solution)/shard_map/all_to_all | solution.py:41
  157.4 0.1 pad_add_fusion.place_ref
  157.5 0.7 order_rows.1
  158.2 0.0 copy-start.1
  158.2 1.4 convolution_convert_fusion
  159.7 18.8 %all-to-all-done.2 = f32[1024,1,128]{2,1,0:T(1,128)} async-done(((f32[1024,1,128]{2,1,0:T(1,128)}), f32[1024,1,128]{2,1,0:T(1,128)}, u32[]{:S(2)}, u32[]{:S(2)}) %all-to-all-start.2) | async-done | bytes 524320 | tf_op jit(solution)/shard_map/all_to_all | solution.py:41
  178.5 2.7 %reduce_sum.29 = f32[]{:T(128)} reduce(f32[1024,1,128]{2,1,0:T(1,128)} %all-to-all-done.2, f32[]{:T(128)} %constant.19.clone.1), dimensions={0,1,2}, to_apply=%region_2.3 | reduce | flops 131071 | bytes 524296 | tf_op jit(solution)/shard_map/reduce_sum | solution.py:117
  182.0 0.7 multiply_subtract_fusion
  (25 shorter events, 0.2 us)
Async XLA Ops:
  0.6 11.2 %copy-start.5 = (bf16[32,2]{0,1:T(2,128)(2,1)S(1)}, bf16[32,2]{0,1:T(2,128)(2,1)}, u32[]{:S(2)}) copy-start(bf16[32,2]{0,1:T(2,128)(2,1)} %param.10) | copy-start | bytes 388
  0.6 11.4 %copy-start.4 = (bf16[32,512]{1,0:T(8,128)(2,1)S(1)}, bf16[32,512]{1,0:T(8,128)(2,1)}, u32[]{:S(2)}) copy-start(bf16[32,512]{1,0:T(8,128)(2,1)} %param.9) | copy-start | bytes 98308
  0.7 32.2 %copy-start = (bf16[256,512]{1,0:T(8,128)(2,1)S(1)}, bf16[256,512]{1,0:T(8,128)(2,1)}, u32[]{:S(2)}) copy-start(bf16[256,512]{1,0:T(8,128)(2,1)} %param.7) | copy-start | bytes 786436
  2.7 51.3 %all-to-all-start = ((bf16[16,128,256]{2,1,0:T(8,128)(2,1)}), bf16[16,128,256]{2,1,0:T(8,128)(2,1)S(1)}, u32[]{:S(2)}, u32[]{:S(2)}) async-start(bf16[16,128,256]{2,1,0:T(8,128)(2,1)} %broadcast_in_dim.8), calls=%async_computation | async-start | bytes 2097152 | tf_op jit(solution)/shard_map/all_to_all | solution.py:41
  12.1 17.5 %collective-permute-start.1 = (bf16[32,512]{1,0:T(8,128)(2,1)S(1)}, bf16[32,512]{1,0:T(8,128)(2,1)S(1)}, u32[]{:S(2)}, u32[]{:S(2)}) collective-permute-start(bf16[32,512]{1,0:T(8,128)(2,1)S(1)} %multiply_convert_fusion), channel_id=1, source_target_pairs={{0,512},{256,768},{512,0},{768,256},{1,513},{257,769},{513,1},{769... | collective-permute-start | bytes 98312 | tf_op jit(solution)/shard_map/ppermute | solution.py:50
  29.6 7.5 %collective-permute-start.2 = (bf16[64,512]{1,0:T(8,128)(2,1)S(1)}, bf16[64,512]{1,0:T(8,128)(2,1)S(1)}, u32[]{:S(2)}, u32[]{:S(2)}) collective-permute-start(bf16[64,512]{1,0:T(8,128)(2,1)S(1)} %pad_maximum_fusion.4), channel_id=1, source_target_pairs={{0,768},{256,0},{512,256},{768,512},{1,769},{257,1},{513,257},{769... | collective-permute-start | bytes 196616 | tf_op jit(solution)/shard_map/ppermute | solution.py:50
  32.9 21.1 %collective-permute-start = (bf16[256,512]{1,0:T(8,128)(2,1)S(1)}, bf16[256,512]{1,0:T(8,128)(2,1)S(1)}, u32[]{:S(2)}, u32[]{:S(2)}) collective-permute-start(bf16[256,512]{1,0:T(8,128)(2,1)S(1)} %copy-done), channel_id=1, source_target_pairs={{0,16},{16,0},{1,17},{17,1},{2,18},{18,2},{3,19},{19,3},{4,20},{20... | collective-permute-start | bytes 786440 | tf_op jit(solution)/shard_map/ppermute | solution.py:45
  37.1 16.8 %collective-permute-start.3 = (bf16[128,512]{1,0:T(8,128)(2,1)S(1)}, bf16[128,512]{1,0:T(8,128)(2,1)S(1)}, u32[]{:S(2)}, u32[]{:S(2)}) collective-permute-start(bf16[128,512]{1,0:T(8,128)(2,1)S(1)} %pad_maximum_fusion.3), channel_id=1, source_target_pairs={{0,128},{32,160},{64,192},{96,224},{128,0},{160,32},{192,64},{224,... | collective-permute-start | bytes 393224 | tf_op jit(solution)/shard_map/ppermute | solution.py:50
  54.1 8.1 %collective-permute-start.4 = (bf16[32,32,256]{2,1,0:T(8,128)(2,1)S(1)}, bf16[32,32,256]{2,1,0:T(8,128)(2,1)S(1)}, u32[]{:S(2)}, u32[]{:S(2)}) collective-permute-start(bf16[32,32,256]{2,1,0:T(8,128)(2,1)S(1)} %dynamic-slice_bitcast_fusion), channel_id=1, source_target_pairs={{0,16},{16,0},{1,17},{17,1},{2,18},{18,2},{3,19},{19,3},{4,20},{20... | collective-permute-start | bytes 1572872 | tf_op jit(solution)/shard_map/ppermute | solution.py:45
  63.6 60.5 %all-to-all-start.1 = ((bf16[32,32,512]{2,1,0:T(8,128)(2,1)}), bf16[32,32,512]{2,1,0:T(8,128)(2,1)S(1)}, u32[]{:S(2)}, u32[]{:S(2)}) async-start(bf16[32,32,512]{2,1,0:T(8,128)(2,1)} %add_convert_fusion), calls=%async_computation.1 | async-start | bytes 2097152 | tf_op jit(solution)/shard_map/all_to_all | solution.py:102
  73.7 36.3 %collective-permute-start.5 = (bf16[256,512]{1,0:T(8,128)(2,1)S(1)}, bf16[256,512]{1,0:T(8,128)(2,1)S(1)}, u32[]{:S(2)}, u32[]{:S(2)}) collective-permute-start(bf16[256,512]{1,0:T(8,128)(2,1)S(1)} %pad_maximum_fusion.2), channel_id=1, source_target_pairs={{0,192},{32,224},{64,0},{96,32},{128,64},{160,96},{192,128},{224,1... | collective-permute-start | bytes 786440 | tf_op jit(solution)/shard_map/ppermute | solution.py:50
  110.0 14.0 %collective-permute-start.6 = (bf16[512,512]{1,0:T(8,128)(2,1)S(1)}, bf16[512,512]{1,0:T(8,128)(2,1)S(1)}, u32[]{:S(2)}, u32[]{:S(2)}) collective-permute-start(bf16[512,512]{1,0:T(8,128)(2,1)S(1)} %pad_maximum_fusion.1), channel_id=1, source_target_pairs={{0,224},{32,0},{64,32},{96,64},{128,96},{160,128},{192,160},{224,1... | collective-permute-start | bytes 1572872 | tf_op jit(solution)/shard_map/ppermute | solution.py:50
  124.2 33.2 %collective-permute-start.7 = (bf16[1024,512]{1,0:T(8,128)(2,1)S(1)}, bf16[1024,512]{1,0:T(8,128)(2,1)S(1)}, u32[]{:S(2)}, u32[]{:S(2)}) collective-permute-start(bf16[1024,512]{1,0:T(8,128)(2,1)S(1)} %pad_maximum_fusion.mine_ref), channel_id=1, source_target_pairs={{0,16},{16,0},{1,17},{17,1},{2,18},{18,2},{3,19},{19,3},{4,20},{20... | collective-permute-start | bytes 3145736 | tf_op jit(solution)/shard_map/ppermute | solution.py:45
  129.5 49.0 %all-to-all-start.2 = ((f32[1024,1,128]{2,1,0:T(1,128)}), f32[1024,1,128]{2,1,0:T(1,128)}, u32[]{:S(2)}, u32[]{:S(2)}) async-start(f32[1024,1,128]{2,1,0:T(1,128)} %broadcast_in_dim.21), calls=%async_computation.2 | async-start | bytes 1048576 | tf_op jit(solution)/shard_map/all_to_all | solution.py:41
  158.2 23.8 %copy-start.1 = (f32[32,512]{1,0:T(8,128)S(1)}, f32[32,512]{1,0:T(8,128)}, u32[]{:S(2)}) copy-start(f32[32,512]{1,0:T(8,128)} %param.11) | copy-start | bytes 196612
  158.2 23.7 %copy-start.2 = (f32[32,512]{1,0:T(8,128)S(1)}, f32[32,512]{1,0:T(8,128)}, u32[]{:S(2)}) copy-start(f32[32,512]{1,0:T(8,128)} %param.12) | copy-start | bytes 196612
  158.2 23.7 %copy-start.3 = (f32[32,512]{1,0:T(8,128)S(1)}, f32[32,512]{1,0:T(8,128)}, u32[]{:S(2)}) copy-start(f32[32,512]{1,0:T(8,128)} %param.13) | copy-start | bytes 196612

commit v3 on v2

--- a/solution.py
+++ b/solution.py
@@ -7,6 +7,7 @@
 from jax.experimental.pallas import tpu as pltpu
 from jax.sharding import Mesh
 from jax.sharding import PartitionSpec as P
+
 
 BLOCK = 256
 CLIP = 2048
@@ -25,7 +26,6 @@
 CHIPS = ("xh", "z")
 N_CHIPS = 32
 N_GROUP = 16
-N_ALL = 1024
 
 
 def dequantize(codes, scales):
@@ -50,11 +50,13 @@
     return lax.ppermute(block, axis, [(i, (i - distance) % size) for i in range(size)])
 
 
-def collect(block, order, axis, distances):
+def collect(block, order, axis, distances, share=1):
+    part = block[: block.shape[0] // share]
+    near = order[: len(order) // share]
     for d in distances:
-        block = jnp.concatenate([block, fetch(block, axis, d)], axis=0)
-        order = order + [(x + d, z) if axis == "xh" else (x, z + d) for x, z in order]
-    return block, order
+        step = d % SIZES[axis]
+        order = order + [(x + step, z) if axis == "xh" else (x, z + step) for x, z in near]
+    return jnp.concatenate([block] + [fetch(part, axis, d) for d in distances], axis=0), order
 
 
 def order_rows_kernel(order, rows, place_ref, mine_ref, other_ref, out_ref):
@@ -84,36 +86,39 @@
     )(place.astype(jnp.int32), mine, other)
 
 
-def shards(layer_input, kv_cotangent, weight_codes, block_scales, master, moment_one, moment_two):
+def work(layer_input, kv_cotangent, weight_codes, block_scales, master, moment_one, moment_two):
     core = lax.axis_index("core")
     rows, cols = weight_codes.shape
     tokens = kv_cotangent.shape[0]
 
     cot = spread(kv_cotangent.T, GROUP, N_GROUP).reshape(-1, tokens)
     input_other = swap_cores(layer_input)
-    mine, order = collect(dequantize(weight_codes, block_scales), [(0, 0)], "xh", (2, 1))
-    mine, order = collect(mine, order, "z", (4,))
+    mine, order = collect(dequantize(weight_codes, block_scales), [(0, 0)], "xh", (2,))
+    mine, order = collect(mine, order, "xh", (1,))
     cot, input_other, mine = lax.optimization_barrier((cot, input_other, mine))
+
     halves = cot.reshape(N_CHIPS, 2, rows, tokens)
     keep = lax.dynamic_index_in_dim(halves, core, 1, keepdims=False)
     cot_other = swap_cores(lax.dynamic_index_in_dim(halves, 1 - core, 1, keepdims=False))
     pair = jnp.einsum("crt,td->crd", keep, layer_input, preferred_element_type=jnp.float32)
     pair += jnp.einsum("crt,td->crd", cot_other, input_other, preferred_element_type=jnp.float32)
     pieces = lax.all_to_all(pair.astype(jnp.bfloat16), CHIPS, 0, 0)
-    mine, order = collect(mine, order, "z", (2, 1))
+    mine, order = collect(mine, order, "z", (4,))
+    mine, order = collect(mine, order, "z", (2, -2), share=2)
     pieces, mine = lax.optimization_barrier((pieces, mine))
     gradient = jnp.sum(pieces.astype(jnp.float32), axis=0)
 
-    squares = jnp.sum(gradient * gradient, axis=0, keepdims=True)
+    squares = jnp.sum((gradient * gradient).reshape(-1, 8, cols), axis=0)
     squares = sum(squares[:, i : i + 128] for i in range(0, cols, 128))
-    squares = spread(squares, DP + GROUP, N_ALL)
-
+    squares = spread(squares, CHIPS, N_CHIPS)
+    mine, order = collect(mine, order, "z", (1, -1), share=2)
+    squares, mine = lax.optimization_barrier((squares, mine))
+    squares = spread(jnp.sum(squares, axis=0), ("core",) + GROUP, 2 * N_GROUP)
     weight = order_rows(mine, swap_cores(mine), order, rows)
     grad_input = jnp.einsum(
         "ct,cd->td", cot, weight, preferred_element_type=jnp.float32
     ).astype(jnp.bfloat16)
     squares, grad_input = lax.optimization_barrier((squares, grad_input))
-
     square_total = jnp.sum(squares)
     factor = jnp.minimum(1.0, CLIP / (jnp.sqrt(square_total) + EPS_NORM))
     clipped = gradient * factor
@@ -130,7 +135,7 @@
 def solution(mesh):
     fine = Mesh(mesh.devices.reshape(tuple(SIZES.values())), tuple(SIZES))
     return jax.shard_map(
-        shards,
+        work,
         mesh=fine,
         in_specs=(P(DP, GROUP),) * 7,
         out_specs=(P(DP, GROUP),) * 4,

time: 183 us -> 157 us (0.86)
  waiting for transfers between devices: 76.6 us -> 54.3 us
  starting transfers between devices: 93.1 us -> 90 us
    ppermute x5 -> x7, waiting for transfers between devices: 56.7 us -> 36.5 us  [fetch(): lax.ppermute(block, axis, [(i, (i - distance) % size) for i in range(size)])]
    all_to_all x2 -> x3, starting transfers between devices: 37 us -> 24.2 us  [spread(): lax.all_to_all(jnp.broadcast_to(block[None], (count, *block.shape)), axes...]
    all_to_all x1, starting transfers between devices: 10.1 us -> 20.4 us  [work(): pieces = lax.all_to_all(pair.astype(jnp.bfloat16), CHIPS, 0, 0)]
    all_to_all x2 -> x3, waiting for transfers between devices: 18.8 us -> 16.7 us  [spread(): lax.all_to_all(jnp.broadcast_to(block[None], (count, *block.shape)), axes...]
    reduce_sum x3 -> x4, other arithmetic: 2.91 us -> 0.83 us  [the longest x1 0.63 us: work(): square_total = jnp.sum(squares)]
    ppermute x5 -> x7, starting transfers between devices: 31.1 us -> 30.4 us  [fetch(): lax.ppermute(block, axis, [(i, (i - distance) % size) for i in range(size)])]
  transfers between devices with their start and end apart: 11 -> 14, of which waited for: 6 -> 7; matrix products, arithmetic and copies ran while one was open for 2% -> 3% of each run, Pallas kernels for 0% -> 0%
where the time goes in v3:
time: 157 us; the launch traced here: 156 us
  starting transfers between devices  90 us (57%)
  waiting for transfers between devices  54.3 us (35%)
  local copies, waits for them, and re-layouts  3.68 us (2%)
  matrix products  3.27 us (2%)
  other arithmetic  2.7 us (2%)
  between operations  1.72 us (1%)
    ppermute x7, waiting for transfers between devices, fetch(): lax.ppermute(block, axis, [(i, (i - distance) % size) for i in range(size)])  36.5 us
    ppermute x7, starting transfers between devices, fetch(): lax.ppermute(block, axis, [(i, (i - distance) % size) for i in range(size)])  30.4 us
    all_to_all x3, starting transfers between devices, spread(): lax.all_to_all(jnp.broadcast_to(block[None], (count, *block.shape)), axes...  24.2 us
    all_to_all x1, starting transfers between devices, work(): pieces = lax.all_to_all(pair.astype(jnp.bfloat16), CHIPS, 0, 0)  20.4 us
    all_to_all x3, waiting for transfers between devices, spread(): lax.all_to_all(jnp.broadcast_to(block[None], (count, *block.shape)), axes...  16.7 us
    ppermute x3, starting transfers between devices, swap_cores(): return lax.ppermute(block, 'core', [(0, 1), (1, 0)])  15 us
  transfers between devices with their start and end apart: 14, of which 7 were waited for; matrix products, arithmetic and copies ran while one was open for 3% of the time, Pallas kernels for 0%

profile of v3, /device:TPU:1, one launch (start us, length us, event | category | flops | bytes accessed | tf_op | source)
XLA Modules:
  0.0 156.4 jit_solution(10490166769320191577)
XLA Ops:
  0.7 1.0 copy.13
  1.6 1.1 broadcast_in_dim.6
  2.7 9.1 %all-to-all-start = ((bf16[16,128,256]{2,1,0:T(8,128)(2,1)}), bf16[16,128,256]{2,1,0:T(8,128)(2,1)S(1)}, u32[]{:S(2)}, u32[]{:S(2)}) async-start(bf16[16,128,256]{2,1,0:T(8,128)(2,1)} %broadcast_in_dim.6), calls=%async_computation | async-start | bytes 2097152 | tf_op jit(solution)/shard_map/all_to_all | solution.py:41
  12.1 6.2 %collective-permute-start.1 = (bf16[32,512]{1,0:T(8,128)(2,1)S(1)}, bf16[32,512]{1,0:T(8,128)(2,1)S(1)}, u32[]{:S(2)}, u32[]{:S(2)}) collective-permute-start(bf16[32,512]{1,0:T(8,128)(2,1)S(1)} %multiply_convert_fusion), channel_id=1, source_target_pairs={{0,512},{256,768},{512,0},{768,256},{1,513},{257,769},{513,1},{769... | collective-permute-start | bytes 98312 | tf_op jit(solution)/shard_map/ppermute | solution.py:50
  18.3 6.3 %collective-permute-start = (bf16[256,512]{1,0:T(8,128)(2,1)S(1)}, bf16[256,512]{1,0:T(8,128)(2,1)S(1)}, u32[]{:S(2)}, u32[]{:S(2)}) collective-permute-start(bf16[256,512]{1,0:T(8,128)(2,1)S(1)} %copy-done), channel_id=1, source_target_pairs={{0,16},{16,0},{1,17},{17,1},{2,18},{18,2},{3,19},{19,3},{4,20},{20... | collective-permute-start | bytes 786440 | tf_op jit(solution)/shard_map/ppermute | solution.py:45
  24.6 5.0 %collective-permute-done.1 = bf16[32,512]{1,0:T(8,128)(2,1)S(1)} collective-permute-done((bf16[32,512]{1,0:T(8,128)(2,1)S(1)}, bf16[32,512]{1,0:T(8,128)(2,1)S(1)}, u32[]{:S(2)}, u32[]{:S(2)}) %collective-permute-start.1) | collective-permute-done | bytes 32800 | tf_op jit(solution)/shard_map/ppermute | solution.py:50
  29.6 3.2 %collective-permute-start.2 = (bf16[64,512]{1,0:T(8,128)(2,1)S(1)}, bf16[64,512]{1,0:T(8,128)(2,1)S(1)}, u32[]{:S(2)}, u32[]{:S(2)}) collective-permute-start(bf16[64,512]{1,0:T(8,128)(2,1)S(1)} %pad_maximum_fusion.3), channel_id=1, source_target_pairs={{0,768},{256,0},{512,256},{768,512},{1,769},{257,1},{513,257},{769... | collective-permute-start | bytes 196616 | tf_op jit(solution)/shard_map/ppermute | solution.py:50
  32.9 3.7 %collective-permute-done.2 = bf16[64,512]{1,0:T(8,128)(2,1)S(1)} collective-permute-done((bf16[64,512]{1,0:T(8,128)(2,1)S(1)}, bf16[64,512]{1,0:T(8,128)(2,1)S(1)}, u32[]{:S(2)}, u32[]{:S(2)}) %collective-permute-start.2) | collective-permute-done | bytes 65568 | tf_op jit(solution)/shard_map/ppermute | solution.py:50
  36.6 4.3 %collective-permute-start.3 = (bf16[32,32,256]{2,1,0:T(8,128)(2,1)S(1)}, bf16[32,32,256]{2,1,0:T(8,128)(2,1)S(1)}, u32[]{:S(2)}, u32[]{:S(2)}) collective-permute-start(bf16[32,32,256]{2,1,0:T(8,128)(2,1)S(1)} %dynamic-slice_bitcast_fusion), channel_id=1, source_target_pairs={{0,16},{16,0},{1,17},{17,1},{2,18},{18,2},{3,19},{19,3},{4,20},{20... | collective-permute-start | bytes 1572872 | tf_op jit(solution)/shard_map/ppermute | solution.py:45
  41.0 0.4 fusion
  41.4 1.1 collective-permute-done.3
  42.5 1.4 add_convert_fusion
  43.9 20.4 %all-to-all-start.1 = ((bf16[32,32,512]{2,1,0:T(8,128)(2,1)}), bf16[32,32,512]{2,1,0:T(8,128)(2,1)S(1)}, u32[]{:S(2)}, u32[]{:S(2)}) async-start(bf16[32,32,512]{2,1,0:T(8,128)(2,1)} %add_convert_fusion), calls=%async_computation.1 | async-start | bytes 2097152 | tf_op jit(solution)/shard_map/all_to_all | solution.py:105
  64.3 4.0 %collective-permute-start.6 = (bf16[128,512]{1,0:T(8,128)(2,1)S(1)}, bf16[128,512]{1,0:T(8,128)(2,1)S(1)}, u32[]{:S(2)}, u32[]{:S(2)}) collective-permute-start(bf16[128,512]{1,0:T(8,128)(2,1)S(1)} %pad_maximum_fusion.2), channel_id=1, source_target_pairs={{0,64},{32,96},{64,128},{96,160},{128,192},{160,224},{192,0},{224,... | collective-permute-start | bytes 393224 | tf_op jit(solution)/shard_map/ppermute | solution.py:50
  68.3 3.4 %collective-permute-start.5 = (bf16[128,512]{1,0:T(8,128)(2,1)S(1)}, bf16[128,512]{1,0:T(8,128)(2,1)S(1)}, u32[]{:S(2)}, u32[]{:S(2)}) collective-permute-start(bf16[128,512]{1,0:T(8,128)(2,1)S(1)} %pad_maximum_fusion.2), channel_id=1, source_target_pairs={{0,192},{32,224},{64,0},{96,32},{128,64},{160,96},{192,128},{224,1... | collective-permute-start | bytes 393224 | tf_op jit(solution)/shard_map/ppermute | solution.py:50
  71.7 7.0 %collective-permute-start.4 = (bf16[128,512]{1,0:T(8,128)(2,1)S(1)}, bf16[128,512]{1,0:T(8,128)(2,1)S(1)}, u32[]{:S(2)}, u32[]{:S(2)}) collective-permute-start(bf16[128,512]{1,0:T(8,128)(2,1)S(1)} %pad_maximum_fusion.2), channel_id=1, source_target_pairs={{0,128},{32,160},{64,192},{96,224},{128,0},{160,32},{192,64},{224,... | collective-permute-start | bytes 393224 | tf_op jit(solution)/shard_map/ppermute | solution.py:50
  78.8 20.3 %collective-permute-done.6 = bf16[128,512]{1,0:T(8,128)(2,1)S(1)} collective-permute-done((bf16[128,512]{1,0:T(8,128)(2,1)S(1)}, bf16[128,512]{1,0:T(8,128)(2,1)S(1)}, u32[]{:S(2)}, u32[]{:S(2)}) %collective-permute-start.6) | collective-permute-done | bytes 131104 | tf_op jit(solution)/shard_map/ppermute | solution.py:50
  99.0 7.5 %collective-permute-done.4 = bf16[128,512]{1,0:T(8,128)(2,1)S(1)} collective-permute-done((bf16[128,512]{1,0:T(8,128)(2,1)S(1)}, bf16[128,512]{1,0:T(8,128)(2,1)S(1)}, u32[]{:S(2)}, u32[]{:S(2)}) %collective-permute-start.4) | collective-permute-done | bytes 131104 | tf_op jit(solution)/shard_map/ppermute | solution.py:50
  106.7 1.9 %collective-permute-start.8 = (bf16[256,512]{1,0:T(8,128)(2,1)S(1)}, bf16[256,512]{1,0:T(8,128)(2,1)S(1)}, u32[]{:S(2)}, u32[]{:S(2)}) collective-permute-start(bf16[256,512]{1,0:T(8,128)(2,1)S(1)} %slice.19), channel_id=1, source_target_pairs={{0,32},{32,64},{64,96},{96,128},{128,160},{160,192},{192,224},{224... | collective-permute-start | bytes 786440 | tf_op jit(solution)/shard_map/ppermute | solution.py:50
  108.6 4.6 %collective-permute-start.7 = (bf16[256,512]{1,0:T(8,128)(2,1)S(1)}, bf16[256,512]{1,0:T(8,128)(2,1)}, u32[]{:S(2)}, u32[]{:S(2)}) collective-permute-start(bf16[256,512]{1,0:T(8,128)(2,1)S(1)} %slice.19), channel_id=1, source_target_pairs={{0,224},{32,0},{64,32},{96,64},{128,96},{160,128},{192,160},{224,1... | collective-permute-start | bytes 786440 | tf_op jit(solution)/shard_map/ppermute | solution.py:50
  113.4 0.7 broadcast_in_dim.7
  114.0 6.0 %all-to-all-start.2 = ((f32[32,8,128]{2,1,0:T(8,128)}), f32[32,8,128]{2,1,0:T(8,128)S(1)}, u32[]{:S(2)}, u32[]{:S(2)}) async-start(f32[32,8,128]{2,1,0:T(8,128)} %broadcast_in_dim.7), calls=%async_computation.2 | async-start | bytes 262144 | tf_op jit(solution)/shard_map/all_to_all | solution.py:41
  120.0 1.0 pad_maximum_fusion.mine_ref
  121.1 10.5 %all-to-all-done.2 = f32[32,8,128]{2,1,0:T(8,128)S(1)} async-done(((f32[32,8,128]{2,1,0:T(8,128)}), f32[32,8,128]{2,1,0:T(8,128)S(1)}, u32[]{:S(2)}, u32[]{:S(2)}) %all-to-all-start.2) | async-done | bytes 131104 | tf_op jit(solution)/shard_map/all_to_all | solution.py:41
  131.6 4.4 %collective-permute-start.9 = (bf16[1024,512]{1,0:T(8,128)(2,1)S(1)}, bf16[1024,512]{1,0:T(8,128)(2,1)S(1)}, u32[]{:S(2)}, u32[]{:S(2)}) collective-permute-start(bf16[1024,512]{1,0:T(8,128)(2,1)S(1)} %pad_maximum_fusion.mine_ref), channel_id=1, source_target_pairs={{0,16},{16,0},{1,17},{17,1},{2,18},{18,2},{3,19},{19,3},{4,20},{20... | collective-permute-start | bytes 3145736 | tf_op jit(solution)/shard_map/ppermute | solution.py:45
  136.2 0.7 broadcast_in_dim.8
  136.8 9.1 %all-to-all-start.3 = ((f32[32,8,128]{2,1,0:T(8,128)}), f32[32,8,128]{2,1,0:T(8,128)S(1)}, u32[]{:S(2)}, u32[]{:S(2)}) async-start(f32[32,8,128]{2,1,0:T(8,128)} %broadcast_in_dim.8), calls=%async_computation.3 | async-start | bytes 262144 | tf_op jit(solution)/shard_map/all_to_all | solution.py:41
  146.0 0.7 order_rows.1
  146.7 1.4 convolution_convert_fusion
  148.1 6.1 %all-to-all-done.3 = f32[32,8,128]{2,1,0:T(8,128)S(1)} async-done(((f32[32,8,128]{2,1,0:T(8,128)}), f32[32,8,128]{2,1,0:T(8,128)S(1)}, u32[]{:S(2)}, u32[]{:S(2)}) %all-to-all-start.3) | async-done | bytes 131104 | tf_op jit(solution)/shard_map/all_to_all | solution.py:41
  154.3 0.6 reduce_sum.39
  155.7 0.7 multiply_subtract_fusion
  (33 shorter events, 0.7 us)
Async XLA Ops:
  0.6 11.2 %copy-start.5 = (bf16[32,2]{0,1:T(2,128)(2,1)S(1)}, bf16[32,2]{0,1:T(2,128)(2,1)}, u32[]{:S(2)}) copy-start(bf16[32,2]{0,1:T(2,128)(2,1)} %param.10) | copy-start | bytes 388
  0.6 11.4 %copy-start.4 = (bf16[32,512]{1,0:T(8,128)(2,1)S(1)}, bf16[32,512]{1,0:T(8,128)(2,1)}, u32[]{:S(2)}) copy-start(bf16[32,512]{1,0:T(8,128)(2,1)} %param.9) | copy-start | bytes 98308
  0.7 17.7 %copy-start = (bf16[256,512]{1,0:T(8,128)(2,1)S(1)}, bf16[256,512]{1,0:T(8,128)(2,1)}, u32[]{:S(2)}) copy-start(bf16[256,512]{1,0:T(8,128)(2,1)} %param.7) | copy-start | bytes 786436
  2.7 33.8 %all-to-all-start = ((bf16[16,128,256]{2,1,0:T(8,128)(2,1)}), bf16[16,128,256]{2,1,0:T(8,128)(2,1)S(1)}, u32[]{:S(2)}, u32[]{:S(2)}) async-start(bf16[16,128,256]{2,1,0:T(8,128)(2,1)} %broadcast_in_dim.6), calls=%async_computation | async-start | bytes 2097152 | tf_op jit(solution)/shard_map/all_to_all | solution.py:41
  12.1 17.5 %collective-permute-start.1 = (bf16[32,512]{1,0:T(8,128)(2,1)S(1)}, bf16[32,512]{1,0:T(8,128)(2,1)S(1)}, u32[]{:S(2)}, u32[]{:S(2)}) collective-permute-start(bf16[32,512]{1,0:T(8,128)(2,1)S(1)} %multiply_convert_fusion), channel_id=1, source_target_pairs={{0,512},{256,768},{512,0},{768,256},{1,513},{257,769},{513,1},{769... | collective-permute-start | bytes 98312 | tf_op jit(solution)/shard_map/ppermute | solution.py:50
  18.3 18.2 %collective-permute-start = (bf16[256,512]{1,0:T(8,128)(2,1)S(1)}, bf16[256,512]{1,0:T(8,128)(2,1)S(1)}, u32[]{:S(2)}, u32[]{:S(2)}) collective-permute-start(bf16[256,512]{1,0:T(8,128)(2,1)S(1)} %copy-done), channel_id=1, source_target_pairs={{0,16},{16,0},{1,17},{17,1},{2,18},{18,2},{3,19},{19,3},{4,20},{20... | collective-permute-start | bytes 786440 | tf_op jit(solution)/shard_map/ppermute | solution.py:45
  29.6 6.9 %collective-permute-start.2 = (bf16[64,512]{1,0:T(8,128)(2,1)S(1)}, bf16[64,512]{1,0:T(8,128)(2,1)S(1)}, u32[]{:S(2)}, u32[]{:S(2)}) collective-permute-start(bf16[64,512]{1,0:T(8,128)(2,1)S(1)} %pad_maximum_fusion.3), channel_id=1, source_target_pairs={{0,768},{256,0},{512,256},{768,512},{1,769},{257,1},{513,257},{769... | collective-permute-start | bytes 196616 | tf_op jit(solution)/shard_map/ppermute | solution.py:50
  36.6 5.9 %collective-permute-start.3 = (bf16[32,32,256]{2,1,0:T(8,128)(2,1)S(1)}, bf16[32,32,256]{2,1,0:T(8,128)(2,1)S(1)}, u32[]{:S(2)}, u32[]{:S(2)}) collective-permute-start(bf16[32,32,256]{2,1,0:T(8,128)(2,1)S(1)} %dynamic-slice_bitcast_fusion), channel_id=1, source_target_pairs={{0,16},{16,0},{1,17},{17,1},{2,18},{18,2},{3,19},{19,3},{4,20},{20... | collective-permute-start | bytes 1572872 | tf_op jit(solution)/shard_map/ppermute | solution.py:45
  43.9 62.7 %all-to-all-start.1 = ((bf16[32,32,512]{2,1,0:T(8,128)(2,1)}), bf16[32,32,512]{2,1,0:T(8,128)(2,1)S(1)}, u32[]{:S(2)}, u32[]{:S(2)}) async-start(bf16[32,32,512]{2,1,0:T(8,128)(2,1)} %add_convert_fusion), calls=%async_computation.1 | async-start | bytes 2097152 | tf_op jit(solution)/shard_map/all_to_all | solution.py:105
  64.3 34.8 %collective-permute-start.6 = (bf16[128,512]{1,0:T(8,128)(2,1)S(1)}, bf16[128,512]{1,0:T(8,128)(2,1)S(1)}, u32[]{:S(2)}, u32[]{:S(2)}) collective-permute-start(bf16[128,512]{1,0:T(8,128)(2,1)S(1)} %pad_maximum_fusion.2), channel_id=1, source_target_pairs={{0,64},{32,96},{64,128},{96,160},{128,192},{160,224},{192,0},{224,... | collective-permute-start | bytes 393224 | tf_op jit(solution)/shard_map/ppermute | solution.py:50
  68.3 30.7 %collective-permute-start.5 = (bf16[128,512]{1,0:T(8,128)(2,1)S(1)}, bf16[128,512]{1,0:T(8,128)(2,1)S(1)}, u32[]{:S(2)}, u32[]{:S(2)}) collective-permute-start(bf16[128,512]{1,0:T(8,128)(2,1)S(1)} %pad_maximum_fusion.2), channel_id=1, source_target_pairs={{0,192},{32,224},{64,0},{96,32},{128,64},{160,96},{192,128},{224,1... | collective-permute-start | bytes 393224 | tf_op jit(solution)/shard_map/ppermute | solution.py:50
  71.7 34.9 %collective-permute-start.4 = (bf16[128,512]{1,0:T(8,128)(2,1)S(1)}, bf16[128,512]{1,0:T(8,128)(2,1)S(1)}, u32[]{:S(2)}, u32[]{:S(2)}) collective-permute-start(bf16[128,512]{1,0:T(8,128)(2,1)S(1)} %pad_maximum_fusion.2), channel_id=1, source_target_pairs={{0,128},{32,160},{64,192},{96,224},{128,0},{160,32},{192,64},{224,... | collective-permute-start | bytes 393224 | tf_op jit(solution)/shard_map/ppermute | solution.py:50
  106.7 13.4 %collective-permute-start.8 = (bf16[256,512]{1,0:T(8,128)(2,1)S(1)}, bf16[256,512]{1,0:T(8,128)(2,1)S(1)}, u32[]{:S(2)}, u32[]{:S(2)}) collective-permute-start(bf16[256,512]{1,0:T(8,128)(2,1)S(1)} %slice.19), channel_id=1, source_target_pairs={{0,32},{32,64},{64,96},{96,128},{128,160},{160,192},{192,224},{224... | collective-permute-start | bytes 786440 | tf_op jit(solution)/shard_map/ppermute | solution.py:50
  108.6 11.4 %collective-permute-start.7 = (bf16[256,512]{1,0:T(8,128)(2,1)S(1)}, bf16[256,512]{1,0:T(8,128)(2,1)}, u32[]{:S(2)}, u32[]{:S(2)}) collective-permute-start(bf16[256,512]{1,0:T(8,128)(2,1)S(1)} %slice.19), channel_id=1, source_target_pairs={{0,224},{32,0},{64,32},{96,64},{128,96},{160,128},{192,160},{224,1... | collective-permute-start | bytes 786440 | tf_op jit(solution)/shard_map/ppermute | solution.py:50
  114.0 17.6 %all-to-all-start.2 = ((f32[32,8,128]{2,1,0:T(8,128)}), f32[32,8,128]{2,1,0:T(8,128)S(1)}, u32[]{:S(2)}, u32[]{:S(2)}) async-start(f32[32,8,128]{2,1,0:T(8,128)} %broadcast_in_dim.7), calls=%async_computation.2 | async-start | bytes 262144 | tf_op jit(solution)/shard_map/all_to_all | solution.py:41
  131.6 14.3 %collective-permute-start.9 = (bf16[1024,512]{1,0:T(8,128)(2,1)S(1)}, bf16[1024,512]{1,0:T(8,128)(2,1)S(1)}, u32[]{:S(2)}, u32[]{:S(2)}) collective-permute-start(bf16[1024,512]{1,0:T(8,128)(2,1)S(1)} %pad_maximum_fusion.mine_ref), channel_id=1, source_target_pairs={{0,16},{16,0},{1,17},{17,1},{2,18},{18,2},{3,19},{19,3},{4,20},{20... | collective-permute-start | bytes 3145736 | tf_op jit(solution)/shard_map/ppermute | solution.py:45
  136.8 17.4 %all-to-all-start.3 = ((f32[32,8,128]{2,1,0:T(8,128)}), f32[32,8,128]{2,1,0:T(8,128)S(1)}, u32[]{:S(2)}, u32[]{:S(2)}) async-start(f32[32,8,128]{2,1,0:T(8,128)} %broadcast_in_dim.8), calls=%async_computation.3 | async-start | bytes 262144 | tf_op jit(solution)/shard_map/all_to_all | solution.py:41
  146.7 9.0 %copy-start.1 = (f32[32,512]{1,0:T(8,128)S(1)}, f32[32,512]{1,0:T(8,128)}, u32[]{:S(2)}) copy-start(f32[32,512]{1,0:T(8,128)} %param.11) | copy-start | bytes 196612
  146.7 9.0 %copy-start.2 = (f32[32,512]{1,0:T(8,128)S(1)}, f32[32,512]{1,0:T(8,128)}, u32[]{:S(2)}) copy-start(f32[32,512]{1,0:T(8,128)} %param.12) | copy-start | bytes 196612
  146.7 9.0 %copy-start.3 = (f32[32,512]{1,0:T(8,128)S(1)}, f32[32,512]{1,0:T(8,128)}, u32[]{:S(2)}) copy-start(f32[32,512]{1,0:T(8,128)} %param.13) | copy-start | bytes 196612

commit v4 on v3

--- a/solution.py
+++ b/solution.py
@@ -50,13 +50,16 @@
     return lax.ppermute(block, axis, [(i, (i - distance) % size) for i in range(size)])
 
 
-def collect(block, order, axis, distances, share=1):
-    part = block[: block.shape[0] // share]
-    near = order[: len(order) // share]
-    for d in distances:
-        step = d % SIZES[axis]
-        order = order + [(x + step, z) if axis == "xh" else (x, z + step) for x, z in near]
-    return jnp.concatenate([block] + [fetch(part, axis, d) for d in distances], axis=0), order
+def collect(block, order, axis, takes, lead=0):
+    rows = block.shape[0] // len(order)
+    parts, places = [], []
+    for distance, first, last in takes:
+        step = distance % SIZES[axis]
+        parts.append(fetch(block[first * rows : last * rows], axis, distance))
+        places.append([(x + step, z) if axis == "xh" else (x, z + step) for x, z in order[first:last]])
+    parts.insert(lead, block)
+    places.insert(lead, order)
+    return jnp.concatenate(parts, axis=0), sum(places, [])
 
 
 def order_rows_kernel(order, rows, place_ref, mine_ref, other_ref, out_ref):
@@ -93,8 +96,8 @@
 
     cot = spread(kv_cotangent.T, GROUP, N_GROUP).reshape(-1, tokens)
     input_other = swap_cores(layer_input)
-    mine, order = collect(dequantize(weight_codes, block_scales), [(0, 0)], "xh", (2,))
-    mine, order = collect(mine, order, "xh", (1,))
+    mine, order = collect(dequantize(weight_codes, block_scales), [(0, 0)], "xh", ((2, 0, 1),))
+    mine, order = collect(mine, order, "xh", ((1, 0, 2),))
     cot, input_other, mine = lax.optimization_barrier((cot, input_other, mine))
 
     halves = cot.reshape(N_CHIPS, 2, rows, tokens)
@@ -103,15 +106,14 @@
     pair = jnp.einsum("crt,td->crd", keep, layer_input, preferred_element_type=jnp.float32)
     pair += jnp.einsum("crt,td->crd", cot_other, input_other, preferred_element_type=jnp.float32)
     pieces = lax.all_to_all(pair.astype(jnp.bfloat16), CHIPS, 0, 0)
-    mine, order = collect(mine, order, "z", (4,))
-    mine, order = collect(mine, order, "z", (2, -2), share=2)
+    mine, order = collect(mine, order, "z", ((2, 0, 4), (-2, 0, 4)), lead=1)
     pieces, mine = lax.optimization_barrier((pieces, mine))
     gradient = jnp.sum(pieces.astype(jnp.float32), axis=0)
 
     squares = jnp.sum((gradient * gradient).reshape(-1, 8, cols), axis=0)
     squares = sum(squares[:, i : i + 128] for i in range(0, cols, 128))
     squares = spread(squares, CHIPS, N_CHIPS)
-    mine, order = collect(mine, order, "z", (1, -1), share=2)
+    mine, order = collect(mine, order, "z", ((1, 0, 8), (-1, 4, 12), (2, 0, 4)))
     squares, mine = lax.optimization_barrier((squares, mine))
     squares = spread(jnp.sum(squares, axis=0), ("core",) + GROUP, 2 * N_GROUP)
     weight = order_rows(mine, swap_cores(mine), order, rows)

time: 157 us -> 155 us (0.987)
  starting transfers between devices: 90 us -> 86.4 us
    ppermute x7, starting transfers between devices: 30.4 us -> 25.8 us  [fetch(): lax.ppermute(block, axis, [(i, (i - distance) % size) for i in range(size)])]
  transfers between devices with their start and end apart: 14 -> 14, of which waited for: 7 -> 6; matrix products, arithmetic and copies ran while one was open for 3% -> 3% of each run, Pallas kernels for 0% -> 0%
where the time goes in v4:
time: 155 us; the launch traced here: 154 us
  starting transfers between devices  86.4 us (56%)
  waiting for transfers between devices  55.3 us (36%)
  local copies, waits for them, and re-layouts  3.72 us (2%)
  matrix products  3.27 us (2%)
  other arithmetic  2.77 us (2%)
  between operations  1.74 us (1%)
    ppermute x7, waiting for transfers between devices, fetch(): lax.ppermute(block, axis, [(i, (i - distance) % size) for i in range(size)])  37.7 us
    ppermute x7, starting transfers between devices, fetch(): lax.ppermute(block, axis, [(i, (i - distance) % size) for i in range(size)])  25.8 us
    all_to_all x3, starting transfers between devices, spread(): lax.all_to_all(jnp.broadcast_to(block[None], (count, *block.shape)), axes...  24.8 us
    all_to_all x1, starting transfers between devices, work(): pieces = lax.all_to_all(pair.astype(jnp.bfloat16), CHIPS, 0, 0)  20.4 us
    all_to_all x3, waiting for transfers between devices, spread(): lax.all_to_all(jnp.broadcast_to(block[None], (count, *block.shape)), axes...  16.5 us
    ppermute x3, starting transfers between devices, swap_cores(): return lax.ppermute(block, 'core', [(0, 1), (1, 0)])  15.4 us
  transfers between devices with their start and end apart: 14, of which 6 were waited for; matrix products, arithmetic and copies ran while one was open for 3% of the time, Pallas kernels for 0%

profile of v4, /device:TPU:1, one launch (start us, length us, event | category | flops | bytes accessed | tf_op | source)
XLA Modules:
  0.0 153.8 jit_solution(9998009322221995775)
XLA Ops:
  0.7 1.0 copy.13
  1.6 1.1 broadcast_in_dim.6
  2.7 9.1 %all-to-all-start = ((bf16[16,128,256]{2,1,0:T(8,128)(2,1)}), bf16[16,128,256]{2,1,0:T(8,128)(2,1)S(1)}, u32[]{:S(2)}, u32[]{:S(2)}) async-start(bf16[16,128,256]{2,1,0:T(8,128)(2,1)} %broadcast_in_dim.6), calls=%async_computation | async-start | bytes 2097152 | tf_op jit(solution)/shard_map/all_to_all | solution.py:41
  12.1 6.2 %collective-permute-start.1 = (bf16[32,512]{1,0:T(8,128)(2,1)S(1)}, bf16[32,512]{1,0:T(8,128)(2,1)S(1)}, u32[]{:S(2)}, u32[]{:S(2)}) collective-permute-start(bf16[32,512]{1,0:T(8,128)(2,1)S(1)} %multiply_convert_fusion), channel_id=1, source_target_pairs={{0,512},{256,768},{512,0},{768,256},{1,513},{257,769},{513,1},{769... | collective-permute-start | bytes 98312 | tf_op jit(solution)/shard_map/ppermute | solution.py:50
  18.3 6.3 %collective-permute-start = (bf16[256,512]{1,0:T(8,128)(2,1)S(1)}, bf16[256,512]{1,0:T(8,128)(2,1)S(1)}, u32[]{:S(2)}, u32[]{:S(2)}) collective-permute-start(bf16[256,512]{1,0:T(8,128)(2,1)S(1)} %copy-done), channel_id=1, source_target_pairs={{0,16},{16,0},{1,17},{17,1},{2,18},{18,2},{3,19},{19,3},{4,20},{20... | collective-permute-start | bytes 786440 | tf_op jit(solution)/shard_map/ppermute | solution.py:45
  24.6 5.0 %collective-permute-done.1 = bf16[32,512]{1,0:T(8,128)(2,1)S(1)} collective-permute-done((bf16[32,512]{1,0:T(8,128)(2,1)S(1)}, bf16[32,512]{1,0:T(8,128)(2,1)S(1)}, u32[]{:S(2)}, u32[]{:S(2)}) %collective-permute-start.1) | collective-permute-done | bytes 32800 | tf_op jit(solution)/shard_map/ppermute | solution.py:50
  29.6 3.2 %collective-permute-start.2 = (bf16[64,512]{1,0:T(8,128)(2,1)S(1)}, bf16[64,512]{1,0:T(8,128)(2,1)S(1)}, u32[]{:S(2)}, u32[]{:S(2)}) collective-permute-start(bf16[64,512]{1,0:T(8,128)(2,1)S(1)} %pad_maximum_fusion.3), channel_id=1, source_target_pairs={{0,768},{256,0},{512,256},{768,512},{1,769},{257,1},{513,257},{769... | collective-permute-start | bytes 196616 | tf_op jit(solution)/shard_map/ppermute | solution.py:50
  32.9 3.7 %collective-permute-done.2 = bf16[64,512]{1,0:T(8,128)(2,1)S(1)} collective-permute-done((bf16[64,512]{1,0:T(8,128)(2,1)S(1)}, bf16[64,512]{1,0:T(8,128)(2,1)S(1)}, u32[]{:S(2)}, u32[]{:S(2)}) %collective-permute-start.2) | collective-permute-done | bytes 65568 | tf_op jit(solution)/shard_map/ppermute | solution.py:50
  36.6 4.3 %collective-permute-start.3 = (bf16[32,32,256]{2,1,0:T(8,128)(2,1)S(1)}, bf16[32,32,256]{2,1,0:T(8,128)(2,1)S(1)}, u32[]{:S(2)}, u32[]{:S(2)}) collective-permute-start(bf16[32,32,256]{2,1,0:T(8,128)(2,1)S(1)} %dynamic-slice_bitcast_fusion), channel_id=1, source_target_pairs={{0,16},{16,0},{1,17},{17,1},{2,18},{18,2},{3,19},{19,3},{4,20},{20... | collective-permute-start | bytes 1572872 | tf_op jit(solution)/shard_map/ppermute | solution.py:45
  41.0 0.4 fusion
  41.4 1.1 collective-permute-done.3
  42.5 1.4 add_convert_fusion
  43.9 20.4 %all-to-all-start.1 = ((bf16[32,32,512]{2,1,0:T(8,128)(2,1)}), bf16[32,32,512]{2,1,0:T(8,128)(2,1)S(1)}, u32[]{:S(2)}, u32[]{:S(2)}) async-start(bf16[32,32,512]{2,1,0:T(8,128)(2,1)} %add_convert_fusion), calls=%async_computation.1 | async-start | bytes 2097152 | tf_op jit(solution)/shard_map/all_to_all | solution.py:108
  64.3 4.0 %collective-permute-start.5 = (bf16[128,512]{1,0:T(8,128)(2,1)S(1)}, bf16[128,512]{1,0:T(8,128)(2,1)S(1)}, u32[]{:S(2)}, u32[]{:S(2)}) collective-permute-start(bf16[128,512]{1,0:T(8,128)(2,1)S(1)} %pad_maximum_fusion.2), channel_id=1, source_target_pairs={{0,64},{32,96},{64,128},{96,160},{128,192},{160,224},{192,0},{224,... | collective-permute-start | bytes 393224 | tf_op jit(solution)/shard_map/ppermute | solution.py:50
  68.3 3.4 %collective-permute-start.4 = (bf16[128,512]{1,0:T(8,128)(2,1)S(1)}, bf16[128,512]{1,0:T(8,128)(2,1)S(1)}, u32[]{:S(2)}, u32[]{:S(2)}) collective-permute-start(bf16[128,512]{1,0:T(8,128)(2,1)S(1)} %pad_maximum_fusion.2), channel_id=1, source_target_pairs={{0,192},{32,224},{64,0},{96,32},{128,64},{160,96},{192,128},{224,1... | collective-permute-start | bytes 393224 | tf_op jit(solution)/shard_map/ppermute | solution.py:50
  71.7 29.0 %collective-permute-done.5 = bf16[128,512]{1,0:T(8,128)(2,1)S(1)} collective-permute-done((bf16[128,512]{1,0:T(8,128)(2,1)S(1)}, bf16[128,512]{1,0:T(8,128)(2,1)S(1)}, u32[]{:S(2)}, u32[]{:S(2)}) %collective-permute-start.5) | collective-permute-done | bytes 131104 | tf_op jit(solution)/shard_map/ppermute | solution.py:50
  100.8 0.2 convert_reduce_fusion
  101.0 2.8 %collective-permute-start.8 = (bf16[128,512]{1,0:T(8,128)(2,1)S(1)}, bf16[128,512]{1,0:T(8,128)(2,1)S(1)}, u32[]{:S(2)}, u32[]{:S(2)}) collective-permute-start(bf16[128,512]{1,0:T(8,128)(2,1)S(1)} %slice.27), channel_id=1, source_target_pairs={{0,192},{32,224},{64,0},{96,32},{128,64},{160,96},{192,128},{224,1... | collective-permute-start | bytes 393224 | tf_op jit(solution)/shard_map/ppermute | solution.py:50
  103.8 3.1 %collective-permute-start.6 = (bf16[256,512]{1,0:T(8,128)(2,1)S(1)}, bf16[256,512]{1,0:T(8,128)(2,1)}, u32[]{:S(2)}, u32[]{:S(2)}) collective-permute-start(bf16[256,512]{1,0:T(8,128)(2,1)S(1)} %get-tuple-element.25), channel_id=1, source_target_pairs={{0,224},{32,0},{64,32},{96,64},{128,96},{160,128},{192,160},{224,1... | collective-permute-start | bytes 786440 | tf_op jit(solution)/shard_map/ppermute | solution.py:50
  106.9 3.1 %collective-permute-start.7 = (bf16[256,512]{1,0:T(8,128)(2,1)S(1)}, bf16[256,512]{1,0:T(8,128)(2,1)}, u32[]{:S(2)}, u32[]{:S(2)}) collective-permute-start(bf16[256,512]{1,0:T(8,128)(2,1)S(1)} %get-tuple-element.26), channel_id=1, source_target_pairs={{0,32},{32,64},{64,96},{96,128},{128,160},{160,192},{192,224},{224... | collective-permute-start | bytes 786440 | tf_op jit(solution)/shard_map/ppermute | solution.py:50
  110.0 0.7 broadcast_in_dim.7
  110.7 7.9 %all-to-all-start.2 = ((f32[32,8,128]{2,1,0:T(8,128)}), f32[32,8,128]{2,1,0:T(8,128)S(1)}, u32[]{:S(2)}, u32[]{:S(2)}) async-start(f32[32,8,128]{2,1,0:T(8,128)} %broadcast_in_dim.7), calls=%async_computation.2 | async-start | bytes 262144 | tf_op jit(solution)/shard_map/all_to_all | solution.py:41
  118.6 1.1 pad_maximum_fusion.mine_ref
  119.7 10.3 %all-to-all-done.2 = f32[32,8,128]{2,1,0:T(8,128)S(1)} async-done(((f32[32,8,128]{2,1,0:T(8,128)}), f32[32,8,128]{2,1,0:T(8,128)S(1)}, u32[]{:S(2)}, u32[]{:S(2)}) %all-to-all-start.2) | async-done | bytes 131104 | tf_op jit(solution)/shard_map/all_to_all | solution.py:41
  130.0 4.8 %collective-permute-start.9 = (bf16[1024,512]{1,0:T(8,128)(2,1)S(1)}, bf16[1024,512]{1,0:T(8,128)(2,1)S(1)}, u32[]{:S(2)}, u32[]{:S(2)}) collective-permute-start(bf16[1024,512]{1,0:T(8,128)(2,1)S(1)} %pad_maximum_fusion.mine_ref), channel_id=1, source_target_pairs={{0,16},{16,0},{1,17},{17,1},{2,18},{18,2},{3,19},{19,3},{4,20},{20... | collective-permute-start | bytes 3145736 | tf_op jit(solution)/shard_map/ppermute | solution.py:45
  134.9 0.7 broadcast_in_dim.8
  135.6 7.8 %all-to-all-start.3 = ((f32[32,8,128]{2,1,0:T(8,128)}), f32[32,8,128]{2,1,0:T(8,128)S(1)}, u32[]{:S(2)}, u32[]{:S(2)}) async-start(f32[32,8,128]{2,1,0:T(8,128)} %broadcast_in_dim.8), calls=%async_computation.3 | async-start | bytes 262144 | tf_op jit(solution)/shard_map/all_to_all | solution.py:41
  143.4 0.7 order_rows.1
  144.2 1.4 convolution_convert_fusion
  145.6 6.1 %all-to-all-done.3 = f32[32,8,128]{2,1,0:T(8,128)S(1)} async-done(((f32[32,8,128]{2,1,0:T(8,128)}), f32[32,8,128]{2,1,0:T(8,128)S(1)}, u32[]{:S(2)}, u32[]{:S(2)}) %all-to-all-start.3) | async-done | bytes 131104 | tf_op jit(solution)/shard_map/all_to_all | solution.py:41
  151.7 0.6 reduce_sum.39
  153.1 0.7 multiply_subtract_fusion
  (34 shorter events, 0.5 us)
Async XLA Ops:
  0.6 11.2 %copy-start.5 = (bf16[32,2]{0,1:T(2,128)(2,1)S(1)}, bf16[32,2]{0,1:T(2,128)(2,1)}, u32[]{:S(2)}) copy-start(bf16[32,2]{0,1:T(2,128)(2,1)} %param.10) | copy-start | bytes 388
  0.6 11.4 %copy-start.4 = (bf16[32,512]{1,0:T(8,128)(2,1)S(1)}, bf16[32,512]{1,0:T(8,128)(2,1)}, u32[]{:S(2)}) copy-start(bf16[32,512]{1,0:T(8,128)(2,1)} %param.9) | copy-start | bytes 98308
  0.7 17.7 %copy-start = (bf16[256,512]{1,0:T(8,128)(2,1)S(1)}, bf16[256,512]{1,0:T(8,128)(2,1)}, u32[]{:S(2)}) copy-start(bf16[256,512]{1,0:T(8,128)(2,1)} %param.7) | copy-start | bytes 786436
  2.7 33.8 %all-to-all-start = ((bf16[16,128,256]{2,1,0:T(8,128)(2,1)}), bf16[16,128,256]{2,1,0:T(8,128)(2,1)S(1)}, u32[]{:S(2)}, u32[]{:S(2)}) async-start(bf16[16,128,256]{2,1,0:T(8,128)(2,1)} %broadcast_in_dim.6), calls=%async_computation | async-start | bytes 2097152 | tf_op jit(solution)/shard_map/all_to_all | solution.py:41
  12.1 17.5 %collective-permute-start.1 = (bf16[32,512]{1,0:T(8,128)(2,1)S(1)}, bf16[32,512]{1,0:T(8,128)(2,1)S(1)}, u32[]{:S(2)}, u32[]{:S(2)}) collective-permute-start(bf16[32,512]{1,0:T(8,128)(2,1)S(1)} %multiply_convert_fusion), channel_id=1, source_target_pairs={{0,512},{256,768},{512,0},{768,256},{1,513},{257,769},{513,1},{769... | collective-permute-start | bytes 98312 | tf_op jit(solution)/shard_map/ppermute | solution.py:50
  18.3 18.2 %collective-permute-start = (bf16[256,512]{1,0:T(8,128)(2,1)S(1)}, bf16[256,512]{1,0:T(8,128)(2,1)S(1)}, u32[]{:S(2)}, u32[]{:S(2)}) collective-permute-start(bf16[256,512]{1,0:T(8,128)(2,1)S(1)} %copy-done), channel_id=1, source_target_pairs={{0,16},{16,0},{1,17},{17,1},{2,18},{18,2},{3,19},{19,3},{4,20},{20... | collective-permute-start | bytes 786440 | tf_op jit(solution)/shard_map/ppermute | solution.py:45
  29.6 6.9 %collective-permute-start.2 = (bf16[64,512]{1,0:T(8,128)(2,1)S(1)}, bf16[64,512]{1,0:T(8,128)(2,1)S(1)}, u32[]{:S(2)}, u32[]{:S(2)}) collective-permute-start(bf16[64,512]{1,0:T(8,128)(2,1)S(1)} %pad_maximum_fusion.3), channel_id=1, source_target_pairs={{0,768},{256,0},{512,256},{768,512},{1,769},{257,1},{513,257},{769... | collective-permute-start | bytes 196616 | tf_op jit(solution)/shard_map/ppermute | solution.py:50
  36.6 5.9 %collective-permute-start.3 = (bf16[32,32,256]{2,1,0:T(8,128)(2,1)S(1)}, bf16[32,32,256]{2,1,0:T(8,128)(2,1)S(1)}, u32[]{:S(2)}, u32[]{:S(2)}) collective-permute-start(bf16[32,32,256]{2,1,0:T(8,128)(2,1)S(1)} %dynamic-slice_bitcast_fusion), channel_id=1, source_target_pairs={{0,16},{16,0},{1,17},{17,1},{2,18},{18,2},{3,19},{19,3},{4,20},{20... | collective-permute-start | bytes 1572872 | tf_op jit(solution)/shard_map/ppermute | solution.py:45
  43.9 56.9 %all-to-all-start.1 = ((bf16[32,32,512]{2,1,0:T(8,128)(2,1)}), bf16[32,32,512]{2,1,0:T(8,128)(2,1)S(1)}, u32[]{:S(2)}, u32[]{:S(2)}) async-start(bf16[32,32,512]{2,1,0:T(8,128)(2,1)} %add_convert_fusion), calls=%async_computation.1 | async-start | bytes 2097152 | tf_op jit(solution)/shard_map/all_to_all | solution.py:108
  64.3 36.4 %collective-permute-start.5 = (bf16[128,512]{1,0:T(8,128)(2,1)S(1)}, bf16[128,512]{1,0:T(8,128)(2,1)S(1)}, u32[]{:S(2)}, u32[]{:S(2)}) collective-permute-start(bf16[128,512]{1,0:T(8,128)(2,1)S(1)} %pad_maximum_fusion.2), channel_id=1, source_target_pairs={{0,64},{32,96},{64,128},{96,160},{128,192},{160,224},{192,0},{224,... | collective-permute-start | bytes 393224 | tf_op jit(solution)/shard_map/ppermute | solution.py:50
  68.3 32.4 %collective-permute-start.4 = (bf16[128,512]{1,0:T(8,128)(2,1)S(1)}, bf16[128,512]{1,0:T(8,128)(2,1)S(1)}, u32[]{:S(2)}, u32[]{:S(2)}) collective-permute-start(bf16[128,512]{1,0:T(8,128)(2,1)S(1)} %pad_maximum_fusion.2), channel_id=1, source_target_pairs={{0,192},{32,224},{64,0},{96,32},{128,64},{160,96},{192,128},{224,1... | collective-permute-start | bytes 393224 | tf_op jit(solution)/shard_map/ppermute | solution.py:50
  101.0 17.6 %collective-permute-start.8 = (bf16[128,512]{1,0:T(8,128)(2,1)S(1)}, bf16[128,512]{1,0:T(8,128)(2,1)S(1)}, u32[]{:S(2)}, u32[]{:S(2)}) collective-permute-start(bf16[128,512]{1,0:T(8,128)(2,1)S(1)} %slice.27), channel_id=1, source_target_pairs={{0,192},{32,224},{64,0},{96,32},{128,64},{160,96},{192,128},{224,1... | collective-permute-start | bytes 393224 | tf_op jit(solution)/shard_map/ppermute | solution.py:50
  103.8 14.8 %collective-permute-start.6 = (bf16[256,512]{1,0:T(8,128)(2,1)S(1)}, bf16[256,512]{1,0:T(8,128)(2,1)}, u32[]{:S(2)}, u32[]{:S(2)}) collective-permute-start(bf16[256,512]{1,0:T(8,128)(2,1)S(1)} %get-tuple-element.25), channel_id=1, source_target_pairs={{0,224},{32,0},{64,32},{96,64},{128,96},{160,128},{192,160},{224,1... | collective-permute-start | bytes 786440 | tf_op jit(solution)/shard_map/ppermute | solution.py:50
  106.9 11.7 %collective-permute-start.7 = (bf16[256,512]{1,0:T(8,128)(2,1)S(1)}, bf16[256,512]{1,0:T(8,128)(2,1)}, u32[]{:S(2)}, u32[]{:S(2)}) collective-permute-start(bf16[256,512]{1,0:T(8,128)(2,1)S(1)} %get-tuple-element.26), channel_id=1, source_target_pairs={{0,32},{32,64},{64,96},{96,128},{128,160},{160,192},{192,224},{224... | collective-permute-start | bytes 786440 | tf_op jit(solution)/shard_map/ppermute | solution.py:50
  110.7 19.4 %all-to-all-start.2 = ((f32[32,8,128]{2,1,0:T(8,128)}), f32[32,8,128]{2,1,0:T(8,128)S(1)}, u32[]{:S(2)}, u32[]{:S(2)}) async-start(f32[32,8,128]{2,1,0:T(8,128)} %broadcast_in_dim.7), calls=%async_computation.2 | async-start | bytes 262144 | tf_op jit(solution)/shard_map/all_to_all | solution.py:41
  130.0 13.4 %collective-permute-start.9 = (bf16[1024,512]{1,0:T(8,128)(2,1)S(1)}, bf16[1024,512]{1,0:T(8,128)(2,1)S(1)}, u32[]{:S(2)}, u32[]{:S(2)}) collective-permute-start(bf16[1024,512]{1,0:T(8,128)(2,1)S(1)} %pad_maximum_fusion.mine_ref), channel_id=1, source_target_pairs={{0,16},{16,0},{1,17},{17,1},{2,18},{18,2},{3,19},{19,3},{4,20},{20... | collective-permute-start | bytes 3145736 | tf_op jit(solution)/shard_map/ppermute | solution.py:45
  135.6 16.2 %all-to-all-start.3 = ((f32[32,8,128]{2,1,0:T(8,128)}), f32[32,8,128]{2,1,0:T(8,128)S(1)}, u32[]{:S(2)}, u32[]{:S(2)}) async-start(f32[32,8,128]{2,1,0:T(8,128)} %broadcast_in_dim.8), calls=%async_computation.3 | async-start | bytes 262144 | tf_op jit(solution)/shard_map/all_to_all | solution.py:41
  144.1 9.0 %copy-start.1 = (f32[32,512]{1,0:T(8,128)S(1)}, f32[32,512]{1,0:T(8,128)}, u32[]{:S(2)}) copy-start(f32[32,512]{1,0:T(8,128)} %param.11) | copy-start | bytes 196612
  144.2 9.0 %copy-start.2 = (f32[32,512]{1,0:T(8,128)S(1)}, f32[32,512]{1,0:T(8,128)}, u32[]{:S(2)}) copy-start(f32[32,512]{1,0:T(8,128)} %param.12) | copy-start | bytes 196612
  144.2 9.0 %copy-start.3 = (f32[32,512]{1,0:T(8,128)S(1)}, f32[32,512]{1,0:T(8,128)}, u32[]{:S(2)}) copy-start(f32[32,512]{1,0:T(8,128)} %param.13) | copy-start | bytes 196612

commit v5 on v4

--- a/solution.py
+++ b/solution.py
@@ -96,17 +96,19 @@
 
     cot = spread(kv_cotangent.T, GROUP, N_GROUP).reshape(-1, tokens)
     input_other = swap_cores(layer_input)
-    mine, order = collect(dequantize(weight_codes, block_scales), [(0, 0)], "xh", ((2, 0, 1),))
-    mine, order = collect(mine, order, "xh", ((1, 0, 2),))
-    cot, input_other, mine = lax.optimization_barrier((cot, input_other, mine))
+    mine, order = collect(
+        dequantize(weight_codes, block_scales), [(0, 0)], "xh", ((2, 0, 1), (1, 0, 1), (-1, 0, 1))
+    )
+    cot, input_other, _ = lax.optimization_barrier((cot, input_other, mine))
+    mine, order = collect(mine, order, "z", ((2, 0, 4), (-2, 0, 4)), lead=1)
 
     halves = cot.reshape(N_CHIPS, 2, rows, tokens)
     keep = lax.dynamic_index_in_dim(halves, core, 1, keepdims=False)
-    cot_other = swap_cores(lax.dynamic_index_in_dim(halves, 1 - core, 1, keepdims=False))
+    give = lax.dynamic_index_in_dim(halves, 1 - core, 1, keepdims=False)
+    cot_other = swap_cores(give)
     pair = jnp.einsum("crt,td->crd", keep, layer_input, preferred_element_type=jnp.float32)
     pair += jnp.einsum("crt,td->crd", cot_other, input_other, preferred_element_type=jnp.float32)
     pieces = lax.all_to_all(pair.astype(jnp.bfloat16), CHIPS, 0, 0)
-    mine, order = collect(mine, order, "z", ((2, 0, 4), (-2, 0, 4)), lead=1)
     pieces, mine = lax.optimization_barrier((pieces, mine))
     gradient = jnp.sum(pieces.astype(jnp.float32), axis=0)
 

time: 155 us -> 155 us (level)
  starting transfers between devices: 86.4 us -> 92.5 us
  waiting for transfers between devices: 55.3 us -> 49.2 us
    ppermute x7 -> x8, waiting for transfers between devices: 37.7 us -> 31.4 us  [fetch(): lax.ppermute(block, axis, [(i, (i - distance) % size) for i in range(size)])]
    ppermute x3, starting transfers between devices: 15.4 us -> 18.7 us  [swap_cores(): return lax.ppermute(block, 'core', [(0, 1), (1, 0)])]
    all_to_all x3, starting transfers between devices: 24.8 us -> 27.4 us  [spread(): lax.all_to_all(jnp.broadcast_to(block[None], (count, *block.shape)), axes...]
    ppermute x7 -> x8, starting transfers between devices: 25.8 us -> 27.4 us  [fetch(): lax.ppermute(block, axis, [(i, (i - distance) % size) for i in range(size)])]
  transfers between devices with their start and end apart: 14 -> 15, of which waited for: 6 -> 6; matrix products, arithmetic and copies ran while one was open for 3% -> 3% of each run, Pallas kernels for 0% -> 0%
where the time goes in v5:
time: 155 us; the launch traced here: 154 us
  starting transfers between devices  92.5 us (60%)
  waiting for transfers between devices  49.2 us (32%)
  local copies, waits for them, and re-layouts  3.76 us (2%)
  matrix products  3.28 us (2%)
  other arithmetic  2.73 us (2%)
  between operations  1.79 us (1%)
    ppermute x8, waiting for transfers between devices, fetch(): lax.ppermute(block, axis, [(i, (i - distance) % size) for i in range(size)])  31.4 us
    ppermute x8, starting transfers between devices, fetch(): lax.ppermute(block, axis, [(i, (i - distance) % size) for i in range(size)])  27.4 us
    all_to_all x3, starting transfers between devices, spread(): lax.all_to_all(jnp.broadcast_to(block[None], (count, *block.shape)), axes...  27.4 us
    all_to_all x1, starting transfers between devices, work(): pieces = lax.all_to_all(pair.astype(jnp.bfloat16), CHIPS, 0, 0)  19 us
    ppermute x3, starting transfers between devices, swap_cores(): return lax.ppermute(block, 'core', [(0, 1), (1, 0)])  18.7 us
    all_to_all x3, waiting for transfers between devices, spread(): lax.all_to_all(jnp.broadcast_to(block[None], (count, *block.shape)), axes...  16.7 us
  transfers between devices with their start and end apart: 15, of which 6 were waited for; matrix products, arithmetic and copies ran while one was open for 3% of the time, Pallas kernels for 0%

profile of v5, /device:TPU:1, one launch (start us, length us, event | category | flops | bytes accessed | tf_op | source)
XLA Modules:
  0.0 154.0 jit_solution(17102984166874190259)
XLA Ops:
  0.7 1.0 copy.13
  1.6 1.1 broadcast_in_dim.6
  2.7 9.1 %all-to-all-start = ((bf16[16,128,256]{2,1,0:T(8,128)(2,1)}), bf16[16,128,256]{2,1,0:T(8,128)(2,1)S(1)}, u32[]{:S(2)}, u32[]{:S(2)}) async-start(bf16[16,128,256]{2,1,0:T(8,128)(2,1)} %broadcast_in_dim.6), calls=%async_computation | async-start | bytes 2097152 | tf_op jit(solution)/shard_map/all_to_all | solution.py:41
  11.9 10.6 %collective-permute-start = (bf16[256,512]{1,0:T(8,128)(2,1)S(1)}, bf16[256,512]{1,0:T(8,128)(2,1)S(1)}, u32[]{:S(2)}, u32[]{:S(2)}) collective-permute-start(bf16[256,512]{1,0:T(8,128)(2,1)S(1)} %copy-done), channel_id=1, source_target_pairs={{0,16},{16,0},{1,17},{17,1},{2,18},{18,2},{3,19},{19,3},{4,20},{20... | collective-permute-start | bytes 786440 | tf_op jit(solution)/shard_map/ppermute | solution.py:45
  22.7 1.9 %collective-permute-start.3 = (bf16[32,512]{1,0:T(8,128)(2,1)S(1)}, bf16[32,512]{1,0:T(8,128)(2,1)S(1)}, u32[]{:S(2)}, u32[]{:S(2)}) collective-permute-start(bf16[32,512]{1,0:T(8,128)(2,1)S(1)} %multiply_convert_fusion), channel_id=1, source_target_pairs={{0,256},{256,512},{512,768},{768,0},{1,257},{257,513},{513,769},{7... | collective-permute-start | bytes 98312 | tf_op jit(solution)/shard_map/ppermute | solution.py:50
  24.6 5.5 %collective-permute-start.2 = (bf16[32,512]{1,0:T(8,128)(2,1)S(1)}, bf16[32,512]{1,0:T(8,128)(2,1)S(1)}, u32[]{:S(2)}, u32[]{:S(2)}) collective-permute-start(bf16[32,512]{1,0:T(8,128)(2,1)S(1)} %multiply_convert_fusion), channel_id=1, source_target_pairs={{0,768},{256,0},{512,256},{768,512},{1,769},{257,1},{513,257},{769... | collective-permute-start | bytes 98312 | tf_op jit(solution)/shard_map/ppermute | solution.py:50
  30.1 1.9 %collective-permute-start.1 = (bf16[32,512]{1,0:T(8,128)(2,1)S(1)}, bf16[32,512]{1,0:T(8,128)(2,1)S(1)}, u32[]{:S(2)}, u32[]{:S(2)}) collective-permute-start(bf16[32,512]{1,0:T(8,128)(2,1)S(1)} %multiply_convert_fusion), channel_id=1, source_target_pairs={{0,512},{256,768},{512,0},{768,256},{1,513},{257,769},{513,1},{769... | collective-permute-start | bytes 98312 | tf_op jit(solution)/shard_map/ppermute | solution.py:50
  32.0 6.9 %collective-permute-done.1 = bf16[32,512]{1,0:T(8,128)(2,1)S(1)} collective-permute-done((bf16[32,512]{1,0:T(8,128)(2,1)S(1)}, bf16[32,512]{1,0:T(8,128)(2,1)S(1)}, u32[]{:S(2)}, u32[]{:S(2)}) %collective-permute-start.1) | collective-permute-done | bytes 32800 | tf_op jit(solution)/shard_map/ppermute | solution.py:50
  39.1 3.5 %collective-permute-start.4 = (bf16[32,32,256]{2,1,0:T(8,128)(2,1)S(1)}, bf16[32,32,256]{2,1,0:T(8,128)(2,1)S(1)}, u32[]{:S(2)}, u32[]{:S(2)}) collective-permute-start(bf16[32,32,256]{2,1,0:T(8,128)(2,1)S(1)} %dynamic-slice_bitcast_fusion), channel_id=1, source_target_pairs={{0,16},{16,0},{1,17},{17,1},{2,18},{18,2},{3,19},{19,3},{4,20},{20... | collective-permute-start | bytes 1572872 | tf_op jit(solution)/shard_map/ppermute | solution.py:45
  42.5 0.4 fusion
  43.0 1.1 collective-permute-done.4
  44.0 1.4 add_convert_fusion
  45.5 19.0 %all-to-all-start.1 = ((bf16[32,32,512]{2,1,0:T(8,128)(2,1)}), bf16[32,32,512]{2,1,0:T(8,128)(2,1)S(1)}, u32[]{:S(2)}, u32[]{:S(2)}) async-start(bf16[32,32,512]{2,1,0:T(8,128)(2,1)} %add_convert_fusion), calls=%async_computation.1 | async-start | bytes 2097152 | tf_op jit(solution)/shard_map/all_to_all | solution.py:111
  64.5 5.2 %collective-permute-start.5 = (bf16[128,512]{1,0:T(8,128)(2,1)S(1)}, bf16[128,512]{1,0:T(8,128)(2,1)S(1)}, u32[]{:S(2)}, u32[]{:S(2)}) collective-permute-start(bf16[128,512]{1,0:T(8,128)(2,1)S(1)} %pad_maximum_fusion.1), channel_id=1, source_target_pairs={{0,192},{32,224},{64,0},{96,32},{128,64},{160,96},{192,128},{224,1... | collective-permute-start | bytes 393224 | tf_op jit(solution)/shard_map/ppermute | solution.py:50
  69.8 1.9 %collective-permute-start.6 = (bf16[128,512]{1,0:T(8,128)(2,1)S(1)}, bf16[128,512]{1,0:T(8,128)(2,1)S(1)}, u32[]{:S(2)}, u32[]{:S(2)}) collective-permute-start(bf16[128,512]{1,0:T(8,128)(2,1)S(1)} %pad_maximum_fusion.1), channel_id=1, source_target_pairs={{0,64},{32,96},{64,128},{96,160},{128,192},{160,224},{192,0},{224,... | collective-permute-start | bytes 393224 | tf_op jit(solution)/shard_map/ppermute | solution.py:50
  71.7 23.2 %collective-permute-done.5 = bf16[128,512]{1,0:T(8,128)(2,1)S(1)} collective-permute-done((bf16[128,512]{1,0:T(8,128)(2,1)S(1)}, bf16[128,512]{1,0:T(8,128)(2,1)S(1)}, u32[]{:S(2)}, u32[]{:S(2)}) %collective-permute-start.5) | collective-permute-done | bytes 131104 | tf_op jit(solution)/shard_map/ppermute | solution.py:50
  94.9 1.3 collective-permute-done.6
  96.5 4.6 %collective-permute-start.9 = (bf16[128,512]{1,0:T(8,128)(2,1)S(1)}, bf16[128,512]{1,0:T(8,128)(2,1)S(1)}, u32[]{:S(2)}, u32[]{:S(2)}) collective-permute-start(bf16[128,512]{1,0:T(8,128)(2,1)S(1)} %slice.27), channel_id=1, source_target_pairs={{0,192},{32,224},{64,0},{96,32},{128,64},{160,96},{192,128},{224,1... | collective-permute-start | bytes 393224 | tf_op jit(solution)/shard_map/ppermute | solution.py:50
  101.1 3.2 %collective-permute-start.7 = (bf16[256,512]{1,0:T(8,128)(2,1)S(1)}, bf16[256,512]{1,0:T(8,128)(2,1)}, u32[]{:S(2)}, u32[]{:S(2)}) collective-permute-start(bf16[256,512]{1,0:T(8,128)(2,1)S(1)} %get-tuple-element.23), channel_id=1, source_target_pairs={{0,224},{32,0},{64,32},{96,64},{128,96},{160,128},{192,160},{224,1... | collective-permute-start | bytes 786440 | tf_op jit(solution)/shard_map/ppermute | solution.py:50
  104.4 3.1 %collective-permute-start.8 = (bf16[256,512]{1,0:T(8,128)(2,1)S(1)}, bf16[256,512]{1,0:T(8,128)(2,1)}, u32[]{:S(2)}, u32[]{:S(2)}) collective-permute-start(bf16[256,512]{1,0:T(8,128)(2,1)S(1)} %get-tuple-element.24), channel_id=1, source_target_pairs={{0,32},{32,64},{64,96},{96,128},{128,160},{160,192},{192,224},{224... | collective-permute-start | bytes 786440 | tf_op jit(solution)/shard_map/ppermute | solution.py:50
  107.5 0.7 broadcast_in_dim.7
  108.2 11.7 %all-to-all-start.2 = ((f32[32,8,128]{2,1,0:T(8,128)}), f32[32,8,128]{2,1,0:T(8,128)S(1)}, u32[]{:S(2)}, u32[]{:S(2)}) async-start(f32[32,8,128]{2,1,0:T(8,128)} %broadcast_in_dim.7), calls=%async_computation.2 | async-start | bytes 262144 | tf_op jit(solution)/shard_map/all_to_all | solution.py:41
  119.9 1.1 pad_maximum_fusion.mine_ref
  121.0 10.5 %all-to-all-done.2 = f32[32,8,128]{2,1,0:T(8,128)S(1)} async-done(((f32[32,8,128]{2,1,0:T(8,128)}), f32[32,8,128]{2,1,0:T(8,128)S(1)}, u32[]{:S(2)}, u32[]{:S(2)}) %all-to-all-start.2) | async-done | bytes 131104 | tf_op jit(solution)/shard_map/all_to_all | solution.py:41
  131.6 4.7 %collective-permute-start.10 = (bf16[1024,512]{1,0:T(8,128)(2,1)S(1)}, bf16[1024,512]{1,0:T(8,128)(2,1)S(1)}, u32[]{:S(2)}, u32[]{:S(2)}) collective-permute-start(bf16[1024,512]{1,0:T(8,128)(2,1)S(1)} %pad_maximum_fusion.mine_ref), channel_id=1, source_target_pairs={{0,16},{16,0},{1,17},{17,1},{2,18},{18,2},{3,19},{19,3},{4,20},{20... | collective-permute-start | bytes 3145736 | tf_op jit(solution)/shard_map/ppermute | solution.py:45
  136.4 0.7 broadcast_in_dim.8
  137.1 6.5 %all-to-all-start.3 = ((f32[32,8,128]{2,1,0:T(8,128)}), f32[32,8,128]{2,1,0:T(8,128)S(1)}, u32[]{:S(2)}, u32[]{:S(2)}) async-start(f32[32,8,128]{2,1,0:T(8,128)} %broadcast_in_dim.8), calls=%async_computation.3 | async-start | bytes 262144 | tf_op jit(solution)/shard_map/all_to_all | solution.py:41
  143.6 0.7 order_rows.1
  144.3 1.4 convolution_convert_fusion
  145.8 6.1 %all-to-all-done.3 = f32[32,8,128]{2,1,0:T(8,128)S(1)} async-done(((f32[32,8,128]{2,1,0:T(8,128)}), f32[32,8,128]{2,1,0:T(8,128)S(1)}, u32[]{:S(2)}, u32[]{:S(2)}) %all-to-all-start.3) | async-done | bytes 131104 | tf_op jit(solution)/shard_map/all_to_all | solution.py:41
  151.9 0.6 reduce_sum.39
  153.3 0.7 multiply_subtract_fusion
  (40 shorter events, 0.7 us)
Async XLA Ops:
  0.6 11.2 %copy-start = (bf16[256,512]{1,0:T(8,128)(2,1)S(1)}, bf16[256,512]{1,0:T(8,128)(2,1)}, u32[]{:S(2)}) copy-start(bf16[256,512]{1,0:T(8,128)(2,1)} %param.7) | copy-start | bytes 786436
  0.6 21.8 %copy-start.5 = (bf16[32,2]{0,1:T(2,128)(2,1)S(1)}, bf16[32,2]{0,1:T(2,128)(2,1)}, u32[]{:S(2)}) copy-start(bf16[32,2]{0,1:T(2,128)(2,1)} %param.10) | copy-start | bytes 388
  0.7 22.0 %copy-start.4 = (bf16[32,512]{1,0:T(8,128)(2,1)S(1)}, bf16[32,512]{1,0:T(8,128)(2,1)}, u32[]{:S(2)}) copy-start(bf16[32,512]{1,0:T(8,128)(2,1)} %param.9) | copy-start | bytes 98308
  2.7 36.3 %all-to-all-start = ((bf16[16,128,256]{2,1,0:T(8,128)(2,1)}), bf16[16,128,256]{2,1,0:T(8,128)(2,1)S(1)}, u32[]{:S(2)}, u32[]{:S(2)}) async-start(bf16[16,128,256]{2,1,0:T(8,128)(2,1)} %broadcast_in_dim.6), calls=%async_computation | async-start | bytes 2097152 | tf_op jit(solution)/shard_map/all_to_all | solution.py:41
  11.9 27.1 %collective-permute-start = (bf16[256,512]{1,0:T(8,128)(2,1)S(1)}, bf16[256,512]{1,0:T(8,128)(2,1)S(1)}, u32[]{:S(2)}, u32[]{:S(2)}) collective-permute-start(bf16[256,512]{1,0:T(8,128)(2,1)S(1)} %copy-done), channel_id=1, source_target_pairs={{0,16},{16,0},{1,17},{17,1},{2,18},{18,2},{3,19},{19,3},{4,20},{20... | collective-permute-start | bytes 786440 | tf_op jit(solution)/shard_map/ppermute | solution.py:45
  22.7 9.3 %collective-permute-start.3 = (bf16[32,512]{1,0:T(8,128)(2,1)S(1)}, bf16[32,512]{1,0:T(8,128)(2,1)S(1)}, u32[]{:S(2)}, u32[]{:S(2)}) collective-permute-start(bf16[32,512]{1,0:T(8,128)(2,1)S(1)} %multiply_convert_fusion), channel_id=1, source_target_pairs={{0,256},{256,512},{512,768},{768,0},{1,257},{257,513},{513,769},{7... | collective-permute-start | bytes 98312 | tf_op jit(solution)/shard_map/ppermute | solution.py:50
  24.6 7.4 %collective-permute-start.2 = (bf16[32,512]{1,0:T(8,128)(2,1)S(1)}, bf16[32,512]{1,0:T(8,128)(2,1)S(1)}, u32[]{:S(2)}, u32[]{:S(2)}) collective-permute-start(bf16[32,512]{1,0:T(8,128)(2,1)S(1)} %multiply_convert_fusion), channel_id=1, source_target_pairs={{0,768},{256,0},{512,256},{768,512},{1,769},{257,1},{513,257},{769... | collective-permute-start | bytes 98312 | tf_op jit(solution)/shard_map/ppermute | solution.py:50
  30.1 8.9 %collective-permute-start.1 = (bf16[32,512]{1,0:T(8,128)(2,1)S(1)}, bf16[32,512]{1,0:T(8,128)(2,1)S(1)}, u32[]{:S(2)}, u32[]{:S(2)}) collective-permute-start(bf16[32,512]{1,0:T(8,128)(2,1)S(1)} %multiply_convert_fusion), channel_id=1, source_target_pairs={{0,512},{256,768},{512,0},{768,256},{1,513},{257,769},{513,1},{769... | collective-permute-start | bytes 98312 | tf_op jit(solution)/shard_map/ppermute | solution.py:50
  39.1 5.0 %collective-permute-start.4 = (bf16[32,32,256]{2,1,0:T(8,128)(2,1)S(1)}, bf16[32,32,256]{2,1,0:T(8,128)(2,1)S(1)}, u32[]{:S(2)}, u32[]{:S(2)}) collective-permute-start(bf16[32,32,256]{2,1,0:T(8,128)(2,1)S(1)} %dynamic-slice_bitcast_fusion), channel_id=1, source_target_pairs={{0,16},{16,0},{1,17},{17,1},{2,18},{18,2},{3,19},{19,3},{4,20},{20... | collective-permute-start | bytes 1572872 | tf_op jit(solution)/shard_map/ppermute | solution.py:45
  45.5 50.8 %all-to-all-start.1 = ((bf16[32,32,512]{2,1,0:T(8,128)(2,1)}), bf16[32,32,512]{2,1,0:T(8,128)(2,1)S(1)}, u32[]{:S(2)}, u32[]{:S(2)}) async-start(bf16[32,32,512]{2,1,0:T(8,128)(2,1)} %add_convert_fusion), calls=%async_computation.1 | async-start | bytes 2097152 | tf_op jit(solution)/shard_map/all_to_all | solution.py:111
  64.5 30.4 %collective-permute-start.5 = (bf16[128,512]{1,0:T(8,128)(2,1)S(1)}, bf16[128,512]{1,0:T(8,128)(2,1)S(1)}, u32[]{:S(2)}, u32[]{:S(2)}) collective-permute-start(bf16[128,512]{1,0:T(8,128)(2,1)S(1)} %pad_maximum_fusion.1), channel_id=1, source_target_pairs={{0,192},{32,224},{64,0},{96,32},{128,64},{160,96},{192,128},{224,1... | collective-permute-start | bytes 393224 | tf_op jit(solution)/shard_map/ppermute | solution.py:50
  69.8 26.5 %collective-permute-start.6 = (bf16[128,512]{1,0:T(8,128)(2,1)S(1)}, bf16[128,512]{1,0:T(8,128)(2,1)S(1)}, u32[]{:S(2)}, u32[]{:S(2)}) collective-permute-start(bf16[128,512]{1,0:T(8,128)(2,1)S(1)} %pad_maximum_fusion.1), channel_id=1, source_target_pairs={{0,64},{32,96},{64,128},{96,160},{128,192},{160,224},{192,0},{224,... | collective-permute-start | bytes 393224 | tf_op jit(solution)/shard_map/ppermute | solution.py:50
  96.5 23.4 %collective-permute-start.9 = (bf16[128,512]{1,0:T(8,128)(2,1)S(1)}, bf16[128,512]{1,0:T(8,128)(2,1)S(1)}, u32[]{:S(2)}, u32[]{:S(2)}) collective-permute-start(bf16[128,512]{1,0:T(8,128)(2,1)S(1)} %slice.27), channel_id=1, source_target_pairs={{0,192},{32,224},{64,0},{96,32},{128,64},{160,96},{192,128},{224,1... | collective-permute-start | bytes 393224 | tf_op jit(solution)/shard_map/ppermute | solution.py:50
  101.1 18.8 %collective-permute-start.7 = (bf16[256,512]{1,0:T(8,128)(2,1)S(1)}, bf16[256,512]{1,0:T(8,128)(2,1)}, u32[]{:S(2)}, u32[]{:S(2)}) collective-permute-start(bf16[256,512]{1,0:T(8,128)(2,1)S(1)} %get-tuple-element.23), channel_id=1, source_target_pairs={{0,224},{32,0},{64,32},{96,64},{128,96},{160,128},{192,160},{224,1... | collective-permute-start | bytes 786440 | tf_op jit(solution)/shard_map/ppermute | solution.py:50
  104.4 15.5 %collective-permute-start.8 = (bf16[256,512]{1,0:T(8,128)(2,1)S(1)}, bf16[256,512]{1,0:T(8,128)(2,1)}, u32[]{:S(2)}, u32[]{:S(2)}) collective-permute-start(bf16[256,512]{1,0:T(8,128)(2,1)S(1)} %get-tuple-element.24), channel_id=1, source_target_pairs={{0,32},{32,64},{64,96},{96,128},{128,160},{160,192},{192,224},{224... | collective-permute-start | bytes 786440 | tf_op jit(solution)/shard_map/ppermute | solution.py:50
  108.2 23.4 %all-to-all-start.2 = ((f32[32,8,128]{2,1,0:T(8,128)}), f32[32,8,128]{2,1,0:T(8,128)S(1)}, u32[]{:S(2)}, u32[]{:S(2)}) async-start(f32[32,8,128]{2,1,0:T(8,128)} %broadcast_in_dim.7), calls=%async_computation.2 | async-start | bytes 262144 | tf_op jit(solution)/shard_map/all_to_all | solution.py:41
  131.6 12.0 %collective-permute-start.10 = (bf16[1024,512]{1,0:T(8,128)(2,1)S(1)}, bf16[1024,512]{1,0:T(8,128)(2,1)S(1)}, u32[]{:S(2)}, u32[]{:S(2)}) collective-permute-start(bf16[1024,512]{1,0:T(8,128)(2,1)S(1)} %pad_maximum_fusion.mine_ref), channel_id=1, source_target_pairs={{0,16},{16,0},{1,17},{17,1},{2,18},{18,2},{3,19},{19,3},{4,20},{20... | collective-permute-start | bytes 3145736 | tf_op jit(solution)/shard_map/ppermute | solution.py:45
  137.1 14.9 %all-to-all-start.3 = ((f32[32,8,128]{2,1,0:T(8,128)}), f32[32,8,128]{2,1,0:T(8,128)S(1)}, u32[]{:S(2)}, u32[]{:S(2)}) async-start(f32[32,8,128]{2,1,0:T(8,128)} %broadcast_in_dim.8), calls=%async_computation.3 | async-start | bytes 262144 | tf_op jit(solution)/shard_map/all_to_all | solution.py:41
  144.3 9.0 %copy-start.1 = (f32[32,512]{1,0:T(8,128)S(1)}, f32[32,512]{1,0:T(8,128)}, u32[]{:S(2)}) copy-start(f32[32,512]{1,0:T(8,128)} %param.11) | copy-start | bytes 196612
  144.3 9.0 %copy-start.2 = (f32[32,512]{1,0:T(8,128)S(1)}, f32[32,512]{1,0:T(8,128)}, u32[]{:S(2)}) copy-start(f32[32,512]{1,0:T(8,128)} %param.12) | copy-start | bytes 196612
  144.3 9.0 %copy-start.3 = (f32[32,512]{1,0:T(8,128)S(1)}, f32[32,512]{1,0:T(8,128)}, u32[]{:S(2)}) copy-start(f32[32,512]{1,0:T(8,128)} %param.13) | copy-start | bytes 196612

commit v6 on v5

--- a/solution.py
+++ b/solution.py
@@ -50,16 +50,14 @@
     return lax.ppermute(block, axis, [(i, (i - distance) % size) for i in range(size)])
 
 
-def collect(block, order, axis, takes, lead=0):
+def collect(block, order, axis, takes):
     rows = block.shape[0] // len(order)
-    parts, places = [], []
+    parts, places = [block], list(order)
     for distance, first, last in takes:
         step = distance % SIZES[axis]
         parts.append(fetch(block[first * rows : last * rows], axis, distance))
-        places.append([(x + step, z) if axis == "xh" else (x, z + step) for x, z in order[first:last]])
-    parts.insert(lead, block)
-    places.insert(lead, order)
-    return jnp.concatenate(parts, axis=0), sum(places, [])
+        places += [(x + step, z) if axis == "xh" else (x, z + step) for x, z in order[first:last]]
+    return lax.optimization_barrier(jnp.concatenate(parts, axis=0)), places
 
 
 def order_rows_kernel(order, rows, place_ref, mine_ref, other_ref, out_ref):
@@ -100,7 +98,7 @@
         dequantize(weight_codes, block_scales), [(0, 0)], "xh", ((2, 0, 1), (1, 0, 1), (-1, 0, 1))
     )
     cot, input_other, _ = lax.optimization_barrier((cot, input_other, mine))
-    mine, order = collect(mine, order, "z", ((2, 0, 4), (-2, 0, 4)), lead=1)
+    mine, order = collect(mine, order, "z", ((3, 0, 4), (-3, 0, 4)))
 
     halves = cot.reshape(N_CHIPS, 2, rows, tokens)
     keep = lax.dynamic_index_in_dim(halves, core, 1, keepdims=False)
@@ -115,7 +113,7 @@
     squares = jnp.sum((gradient * gradient).reshape(-1, 8, cols), axis=0)
     squares = sum(squares[:, i : i + 128] for i in range(0, cols, 128))
     squares = spread(squares, CHIPS, N_CHIPS)
-    mine, order = collect(mine, order, "z", ((1, 0, 8), (-1, 4, 12), (2, 0, 4)))
+    mine, order = collect(mine, order, "z", ((1, 0, 12), (-1, 0, 8)))
     squares, mine = lax.optimization_barrier((squares, mine))
     squares = spread(jnp.sum(squares, axis=0), ("core",) + GROUP, 2 * N_GROUP)
     weight = order_rows(mine, swap_cores(mine), order, rows)

time: 155 us -> 154 us (level)
  starting transfers between devices: 92.5 us -> 87.3 us
  waiting for transfers between devices: 49.2 us -> 54 us
    ppermute x8 -> x7, waiting for transfers between devices: 31.4 us -> 36.4 us  [fetch(): lax.ppermute(block, axis, [(i, (i - distance) % size) for i in range(size)])]
    ppermute x8 -> x7, starting transfers between devices: 27.4 us -> 22.9 us  [fetch(): lax.ppermute(block, axis, [(i, (i - distance) % size) for i in range(size)])]
  transfers between devices with their start and end apart: 15 -> 14, of which waited for: 6 -> 5; matrix products, arithmetic and copies ran while one was open for 3% -> 3% of each run, Pallas kernels for 0% -> 0%
where the time goes in v6:
time: 154 us; the launch traced here: 153 us
  starting transfers between devices  87.3 us (57%)
  waiting for transfers between devices  54 us (35%)
  local copies, waits for them, and re-layouts  3.67 us (2%)
  matrix products  3.27 us (2%)
  other arithmetic  2.68 us (2%)
  between operations  1.74 us (1%)
    ppermute x7, waiting for transfers between devices, fetch(): lax.ppermute(block, axis, [(i, (i - distance) % size) for i in range(size)])  36.4 us
    all_to_all x3, starting transfers between devices, spread(): lax.all_to_all(jnp.broadcast_to(block[None], (count, *block.shape)), axes...  27 us
    ppermute x7, starting transfers between devices, fetch(): lax.ppermute(block, axis, [(i, (i - distance) % size) for i in range(size)])  22.9 us
    all_to_all x1, starting transfers between devices, work(): pieces = lax.all_to_all(pair.astype(jnp.bfloat16), CHIPS, 0, 0)  19 us
    ppermute x3, starting transfers between devices, swap_cores(): return lax.ppermute(block, 'core', [(0, 1), (1, 0)])  18.4 us
    all_to_all x3, waiting for transfers between devices, spread(): lax.all_to_all(jnp.broadcast_to(block[None], (count, *block.shape)), axes...  16.6 us
  transfers between devices with their start and end apart: 14, of which 5 were waited for; matrix products, arithmetic and copies ran while one was open for 3% of the time, Pallas kernels for 0%

profile of v6, /device:TPU:1, one launch (start us, length us, event | category | flops | bytes accessed | tf_op | source)
XLA Modules:
  0.0 153.4 jit_solution(10189060541881342895)
XLA Ops:
  0.7 1.0 copy.13
  1.6 1.1 broadcast_in_dim.6
  2.7 9.1 %all-to-all-start = ((bf16[16,128,256]{2,1,0:T(8,128)(2,1)}), bf16[16,128,256]{2,1,0:T(8,128)(2,1)S(1)}, u32[]{:S(2)}, u32[]{:S(2)}) async-start(bf16[16,128,256]{2,1,0:T(8,128)(2,1)} %broadcast_in_dim.6), calls=%async_computation | async-start | bytes 2097152 | tf_op jit(solution)/shard_map/all_to_all | solution.py:41
  11.9 10.6 %collective-permute-start = (bf16[256,512]{1,0:T(8,128)(2,1)S(1)}, bf16[256,512]{1,0:T(8,128)(2,1)S(1)}, u32[]{:S(2)}, u32[]{:S(2)}) collective-permute-start(bf16[256,512]{1,0:T(8,128)(2,1)S(1)} %copy-done), channel_id=1, source_target_pairs={{0,16},{16,0},{1,17},{17,1},{2,18},{18,2},{3,19},{19,3},{4,20},{20... | collective-permute-start | bytes 786440 | tf_op jit(solution)/shard_map/ppermute | solution.py:45
  22.4 0.1 copy.14
  22.7 1.9 %collective-permute-start.3 = (bf16[32,512]{1,0:T(8,128)(2,1)S(1)}, bf16[32,512]{1,0:T(8,128)(2,1)S(1)}, u32[]{:S(2)}, u32[]{:S(2)}) collective-permute-start(bf16[32,512]{1,0:T(8,128)(2,1)S(1)} %multiply_convert_fusion), channel_id=1, source_target_pairs={{0,256},{256,512},{512,768},{768,0},{1,257},{257,513},{513,769},{7... | collective-permute-start | bytes 98312 | tf_op jit(solution)/shard_map/ppermute | solution.py:50
  24.6 5.5 %collective-permute-start.2 = (bf16[32,512]{1,0:T(8,128)(2,1)S(1)}, bf16[32,512]{1,0:T(8,128)(2,1)S(1)}, u32[]{:S(2)}, u32[]{:S(2)}) collective-permute-start(bf16[32,512]{1,0:T(8,128)(2,1)S(1)} %multiply_convert_fusion), channel_id=1, source_target_pairs={{0,768},{256,0},{512,256},{768,512},{1,769},{257,1},{513,257},{769... | collective-permute-start | bytes 98312 | tf_op jit(solution)/shard_map/ppermute | solution.py:50
  30.1 1.9 %collective-permute-start.1 = (bf16[32,512]{1,0:T(8,128)(2,1)S(1)}, bf16[32,512]{1,0:T(8,128)(2,1)S(1)}, u32[]{:S(2)}, u32[]{:S(2)}) collective-permute-start(bf16[32,512]{1,0:T(8,128)(2,1)S(1)} %multiply_convert_fusion), channel_id=1, source_target_pairs={{0,512},{256,768},{512,0},{768,256},{1,513},{257,769},{513,1},{769... | collective-permute-start | bytes 98312 | tf_op jit(solution)/shard_map/ppermute | solution.py:50
  32.0 6.9 %collective-permute-done.1 = bf16[32,512]{1,0:T(8,128)(2,1)S(1)} collective-permute-done((bf16[32,512]{1,0:T(8,128)(2,1)S(1)}, bf16[32,512]{1,0:T(8,128)(2,1)S(1)}, u32[]{:S(2)}, u32[]{:S(2)}) %collective-permute-start.1) | collective-permute-done | bytes 32800 | tf_op jit(solution)/shard_map/ppermute | solution.py:50
  39.1 3.5 %collective-permute-start.4 = (bf16[32,32,256]{2,1,0:T(8,128)(2,1)S(1)}, bf16[32,32,256]{2,1,0:T(8,128)(2,1)S(1)}, u32[]{:S(2)}, u32[]{:S(2)}) collective-permute-start(bf16[32,32,256]{2,1,0:T(8,128)(2,1)S(1)} %dynamic-slice_bitcast_fusion), channel_id=1, source_target_pairs={{0,16},{16,0},{1,17},{17,1},{2,18},{18,2},{3,19},{19,3},{4,20},{20... | collective-permute-start | bytes 1572872 | tf_op jit(solution)/shard_map/ppermute | solution.py:45
  42.5 0.4 fusion
  42.9 1.1 collective-permute-done.4
  44.0 1.4 add_convert_fusion
  45.4 19.0 %all-to-all-start.1 = ((bf16[32,32,512]{2,1,0:T(8,128)(2,1)}), bf16[32,32,512]{2,1,0:T(8,128)(2,1)S(1)}, u32[]{:S(2)}, u32[]{:S(2)}) async-start(bf16[32,32,512]{2,1,0:T(8,128)(2,1)} %add_convert_fusion), calls=%async_computation.1 | async-start | bytes 2097152 | tf_op jit(solution)/shard_map/all_to_all | solution.py:109
  64.5 4.9 %collective-permute-start.6 = (bf16[128,512]{1,0:T(8,128)(2,1)S(1)}, bf16[128,512]{1,0:T(8,128)(2,1)S(1)}, u32[]{:S(2)}, u32[]{:S(2)}) collective-permute-start(bf16[128,512]{1,0:T(8,128)(2,1)S(1)} %pad_maximum_fusion.2), channel_id=1, source_target_pairs={{0,96},{32,128},{64,160},{96,192},{128,224},{160,0},{192,32},{224,... | collective-permute-start | bytes 393224 | tf_op jit(solution)/shard_map/ppermute | solution.py:50
  69.4 3.4 %collective-permute-start.5 = (bf16[128,512]{1,0:T(8,128)(2,1)S(1)}, bf16[128,512]{1,0:T(8,128)(2,1)S(1)}, u32[]{:S(2)}, u32[]{:S(2)}) collective-permute-start(bf16[128,512]{1,0:T(8,128)(2,1)S(1)} %pad_maximum_fusion.2), channel_id=1, source_target_pairs={{0,160},{32,192},{64,224},{96,0},{128,32},{160,64},{192,96},{224,1... | collective-permute-start | bytes 393224 | tf_op jit(solution)/shard_map/ppermute | solution.py:50
  72.8 29.4 %collective-permute-done.6 = bf16[128,512]{1,0:T(8,128)(2,1)S(1)} collective-permute-done((bf16[128,512]{1,0:T(8,128)(2,1)S(1)}, bf16[128,512]{1,0:T(8,128)(2,1)S(1)}, u32[]{:S(2)}, u32[]{:S(2)}) %collective-permute-start.6) | collective-permute-done | bytes 131104 | tf_op jit(solution)/shard_map/ppermute | solution.py:50
  102.3 0.2 convert_reduce_fusion
  102.4 1.9 %collective-permute-start.7 = (bf16[384,512]{1,0:T(8,128)(2,1)S(1)}, bf16[384,512]{1,0:T(8,128)(2,1)S(1)}, u32[]{:S(2)}, u32[]{:S(2)}) collective-permute-start(bf16[384,512]{1,0:T(8,128)(2,1)S(1)} %pad_maximum_fusion.1), channel_id=1, source_target_pairs={{0,224},{32,0},{64,32},{96,64},{128,96},{160,128},{192,160},{224,1... | collective-permute-start | bytes 1179656 | tf_op jit(solution)/shard_map/ppermute | solution.py:50
  104.4 3.4 %collective-permute-start.8 = (bf16[256,512]{1,0:T(8,128)(2,1)S(1)}, bf16[256,512]{1,0:T(8,128)(2,1)}, u32[]{:S(2)}, u32[]{:S(2)}) collective-permute-start(bf16[256,512]{1,0:T(8,128)(2,1)S(1)} %slice.19), channel_id=1, source_target_pairs={{0,32},{32,64},{64,96},{96,128},{128,160},{160,192},{192,224},{224... | collective-permute-start | bytes 786440 | tf_op jit(solution)/shard_map/ppermute | solution.py:50
  107.8 0.7 broadcast_in_dim.7
  108.4 9.5 %all-to-all-start.2 = ((f32[32,8,128]{2,1,0:T(8,128)}), f32[32,8,128]{2,1,0:T(8,128)S(1)}, u32[]{:S(2)}, u32[]{:S(2)}) async-start(f32[32,8,128]{2,1,0:T(8,128)} %broadcast_in_dim.7), calls=%async_computation.2 | async-start | bytes 262144 | tf_op jit(solution)/shard_map/all_to_all | solution.py:41
  118.0 1.0 pad_maximum_fusion.mine_ref
  119.0 10.4 %all-to-all-done.2 = f32[32,8,128]{2,1,0:T(8,128)S(1)} async-done(((f32[32,8,128]{2,1,0:T(8,128)}), f32[32,8,128]{2,1,0:T(8,128)S(1)}, u32[]{:S(2)}, u32[]{:S(2)}) %all-to-all-start.2) | async-done | bytes 131104 | tf_op jit(solution)/shard_map/all_to_all | solution.py:41
  129.5 4.4 %collective-permute-start.9 = (bf16[1024,512]{1,0:T(8,128)(2,1)S(1)}, bf16[1024,512]{1,0:T(8,128)(2,1)S(1)}, u32[]{:S(2)}, u32[]{:S(2)}) collective-permute-start(bf16[1024,512]{1,0:T(8,128)(2,1)S(1)} %pad_maximum_fusion.mine_ref), channel_id=1, source_target_pairs={{0,16},{16,0},{1,17},{17,1},{2,18},{18,2},{3,19},{19,3},{4,20},{20... | collective-permute-start | bytes 3145736 | tf_op jit(solution)/shard_map/ppermute | solution.py:45
  134.0 0.7 broadcast_in_dim.8
  134.6 8.3 %all-to-all-start.3 = ((f32[32,8,128]{2,1,0:T(8,128)}), f32[32,8,128]{2,1,0:T(8,128)S(1)}, u32[]{:S(2)}, u32[]{:S(2)}) async-start(f32[32,8,128]{2,1,0:T(8,128)} %broadcast_in_dim.8), calls=%async_computation.3 | async-start | bytes 262144 | tf_op jit(solution)/shard_map/all_to_all | solution.py:41
  143.0 0.7 order_rows.1
  143.7 1.4 convolution_convert_fusion
  145.2 6.1 %all-to-all-done.3 = f32[32,8,128]{2,1,0:T(8,128)S(1)} async-done(((f32[32,8,128]{2,1,0:T(8,128)}), f32[32,8,128]{2,1,0:T(8,128)S(1)}, u32[]{:S(2)}, u32[]{:S(2)}) %all-to-all-start.3) | async-done | bytes 131104 | tf_op jit(solution)/shard_map/all_to_all | solution.py:41
  151.3 0.6 reduce_sum.39
  152.7 0.7 multiply_subtract_fusion
  (32 shorter events, 0.4 us)
Async XLA Ops:
  0.6 11.2 %copy-start = (bf16[256,512]{1,0:T(8,128)(2,1)S(1)}, bf16[256,512]{1,0:T(8,128)(2,1)}, u32[]{:S(2)}) copy-start(bf16[256,512]{1,0:T(8,128)(2,1)} %param.7) | copy-start | bytes 786436
  0.6 21.8 %copy-start.5 = (bf16[32,2]{0,1:T(2,128)(2,1)S(1)}, bf16[32,2]{0,1:T(2,128)(2,1)}, u32[]{:S(2)}) copy-start(bf16[32,2]{0,1:T(2,128)(2,1)} %param.10) | copy-start | bytes 388
  0.7 22.0 %copy-start.4 = (bf16[32,512]{1,0:T(8,128)(2,1)S(1)}, bf16[32,512]{1,0:T(8,128)(2,1)}, u32[]{:S(2)}) copy-start(bf16[32,512]{1,0:T(8,128)(2,1)} %param.9) | copy-start | bytes 98308
  2.7 36.3 %all-to-all-start = ((bf16[16,128,256]{2,1,0:T(8,128)(2,1)}), bf16[16,128,256]{2,1,0:T(8,128)(2,1)S(1)}, u32[]{:S(2)}, u32[]{:S(2)}) async-start(bf16[16,128,256]{2,1,0:T(8,128)(2,1)} %broadcast_in_dim.6), calls=%async_computation | async-start | bytes 2097152 | tf_op jit(solution)/shard_map/all_to_all | solution.py:41
  11.9 27.1 %collective-permute-start = (bf16[256,512]{1,0:T(8,128)(2,1)S(1)}, bf16[256,512]{1,0:T(8,128)(2,1)S(1)}, u32[]{:S(2)}, u32[]{:S(2)}) collective-permute-start(bf16[256,512]{1,0:T(8,128)(2,1)S(1)} %copy-done), channel_id=1, source_target_pairs={{0,16},{16,0},{1,17},{17,1},{2,18},{18,2},{3,19},{19,3},{4,20},{20... | collective-permute-start | bytes 786440 | tf_op jit(solution)/shard_map/ppermute | solution.py:45
  22.7 9.3 %collective-permute-start.3 = (bf16[32,512]{1,0:T(8,128)(2,1)S(1)}, bf16[32,512]{1,0:T(8,128)(2,1)S(1)}, u32[]{:S(2)}, u32[]{:S(2)}) collective-permute-start(bf16[32,512]{1,0:T(8,128)(2,1)S(1)} %multiply_convert_fusion), channel_id=1, source_target_pairs={{0,256},{256,512},{512,768},{768,0},{1,257},{257,513},{513,769},{7... | collective-permute-start | bytes 98312 | tf_op jit(solution)/shard_map/ppermute | solution.py:50
  24.6 7.4 %collective-permute-start.2 = (bf16[32,512]{1,0:T(8,128)(2,1)S(1)}, bf16[32,512]{1,0:T(8,128)(2,1)S(1)}, u32[]{:S(2)}, u32[]{:S(2)}) collective-permute-start(bf16[32,512]{1,0:T(8,128)(2,1)S(1)} %multiply_convert_fusion), channel_id=1, source_target_pairs={{0,768},{256,0},{512,256},{768,512},{1,769},{257,1},{513,257},{769... | collective-permute-start | bytes 98312 | tf_op jit(solution)/shard_map/ppermute | solution.py:50
  30.1 8.9 %collective-permute-start.1 = (bf16[32,512]{1,0:T(8,128)(2,1)S(1)}, bf16[32,512]{1,0:T(8,128)(2,1)S(1)}, u32[]{:S(2)}, u32[]{:S(2)}) collective-permute-start(bf16[32,512]{1,0:T(8,128)(2,1)S(1)} %multiply_convert_fusion), channel_id=1, source_target_pairs={{0,512},{256,768},{512,0},{768,256},{1,513},{257,769},{513,1},{769... | collective-permute-start | bytes 98312 | tf_op jit(solution)/shard_map/ppermute | solution.py:50
  39.1 5.0 %collective-permute-start.4 = (bf16[32,32,256]{2,1,0:T(8,128)(2,1)S(1)}, bf16[32,32,256]{2,1,0:T(8,128)(2,1)S(1)}, u32[]{:S(2)}, u32[]{:S(2)}) collective-permute-start(bf16[32,32,256]{2,1,0:T(8,128)(2,1)S(1)} %dynamic-slice_bitcast_fusion), channel_id=1, source_target_pairs={{0,16},{16,0},{1,17},{17,1},{2,18},{18,2},{3,19},{19,3},{4,20},{20... | collective-permute-start | bytes 1572872 | tf_op jit(solution)/shard_map/ppermute | solution.py:45
  45.4 56.8 %all-to-all-start.1 = ((bf16[32,32,512]{2,1,0:T(8,128)(2,1)}), bf16[32,32,512]{2,1,0:T(8,128)(2,1)S(1)}, u32[]{:S(2)}, u32[]{:S(2)}) async-start(bf16[32,32,512]{2,1,0:T(8,128)(2,1)} %add_convert_fusion), calls=%async_computation.1 | async-start | bytes 2097152 | tf_op jit(solution)/shard_map/all_to_all | solution.py:109
  64.5 37.7 %collective-permute-start.6 = (bf16[128,512]{1,0:T(8,128)(2,1)S(1)}, bf16[128,512]{1,0:T(8,128)(2,1)S(1)}, u32[]{:S(2)}, u32[]{:S(2)}) collective-permute-start(bf16[128,512]{1,0:T(8,128)(2,1)S(1)} %pad_maximum_fusion.2), channel_id=1, source_target_pairs={{0,96},{32,128},{64,160},{96,192},{128,224},{160,0},{192,32},{224,... | collective-permute-start | bytes 393224 | tf_op jit(solution)/shard_map/ppermute | solution.py:50
  69.4 32.8 %collective-permute-start.5 = (bf16[128,512]{1,0:T(8,128)(2,1)S(1)}, bf16[128,512]{1,0:T(8,128)(2,1)S(1)}, u32[]{:S(2)}, u32[]{:S(2)}) collective-permute-start(bf16[128,512]{1,0:T(8,128)(2,1)S(1)} %pad_maximum_fusion.2), channel_id=1, source_target_pairs={{0,160},{32,192},{64,224},{96,0},{128,32},{160,64},{192,96},{224,1... | collective-permute-start | bytes 393224 | tf_op jit(solution)/shard_map/ppermute | solution.py:50
  102.4 15.6 %collective-permute-start.7 = (bf16[384,512]{1,0:T(8,128)(2,1)S(1)}, bf16[384,512]{1,0:T(8,128)(2,1)S(1)}, u32[]{:S(2)}, u32[]{:S(2)}) collective-permute-start(bf16[384,512]{1,0:T(8,128)(2,1)S(1)} %pad_maximum_fusion.1), channel_id=1, source_target_pairs={{0,224},{32,0},{64,32},{96,64},{128,96},{160,128},{192,160},{224,1... | collective-permute-start | bytes 1179656 | tf_op jit(solution)/shard_map/ppermute | solution.py:50
  104.4 13.6 %collective-permute-start.8 = (bf16[256,512]{1,0:T(8,128)(2,1)S(1)}, bf16[256,512]{1,0:T(8,128)(2,1)}, u32[]{:S(2)}, u32[]{:S(2)}) collective-permute-start(bf16[256,512]{1,0:T(8,128)(2,1)S(1)} %slice.19), channel_id=1, source_target_pairs={{0,32},{32,64},{64,96},{96,128},{128,160},{160,192},{192,224},{224... | collective-permute-start | bytes 786440 | tf_op jit(solution)/shard_map/ppermute | solution.py:50
  108.4 21.0 %all-to-all-start.2 = ((f32[32,8,128]{2,1,0:T(8,128)}), f32[32,8,128]{2,1,0:T(8,128)S(1)}, u32[]{:S(2)}, u32[]{:S(2)}) async-start(f32[32,8,128]{2,1,0:T(8,128)} %broadcast_in_dim.7), calls=%async_computation.2 | async-start | bytes 262144 | tf_op jit(solution)/shard_map/all_to_all | solution.py:41
  129.5 13.5 %collective-permute-start.9 = (bf16[1024,512]{1,0:T(8,128)(2,1)S(1)}, bf16[1024,512]{1,0:T(8,128)(2,1)S(1)}, u32[]{:S(2)}, u32[]{:S(2)}) collective-permute-start(bf16[1024,512]{1,0:T(8,128)(2,1)S(1)} %pad_maximum_fusion.mine_ref), channel_id=1, source_target_pairs={{0,16},{16,0},{1,17},{17,1},{2,18},{18,2},{3,19},{19,3},{4,20},{20... | collective-permute-start | bytes 3145736 | tf_op jit(solution)/shard_map/ppermute | solution.py:45
  134.6 16.7 %all-to-all-start.3 = ((f32[32,8,128]{2,1,0:T(8,128)}), f32[32,8,128]{2,1,0:T(8,128)S(1)}, u32[]{:S(2)}, u32[]{:S(2)}) async-start(f32[32,8,128]{2,1,0:T(8,128)} %broadcast_in_dim.8), calls=%async_computation.3 | async-start | bytes 262144 | tf_op jit(solution)/shard_map/all_to_all | solution.py:41
  143.7 9.0 %copy-start.1 = (f32[32,512]{1,0:T(8,128)S(1)}, f32[32,512]{1,0:T(8,128)}, u32[]{:S(2)}) copy-start(f32[32,512]{1,0:T(8,128)} %param.11) | copy-start | bytes 196612
  143.7 9.0 %copy-start.2 = (f32[32,512]{1,0:T(8,128)S(1)}, f32[32,512]{1,0:T(8,128)}, u32[]{:S(2)}) copy-start(f32[32,512]{1,0:T(8,128)} %param.12) | copy-start | bytes 196612
  143.7 9.0 %copy-start.3 = (f32[32,512]{1,0:T(8,128)S(1)}, f32[32,512]{1,0:T(8,128)}, u32[]{:S(2)}) copy-start(f32[32,512]{1,0:T(8,128)} %param.13) | copy-start | bytes 196612

commit v7 on v6

--- a/solution.py
+++ b/solution.py
@@ -39,6 +39,27 @@
 
 def spread(block, axes, count):
     return lax.all_to_all(jnp.broadcast_to(block[None], (count, *block.shape)), axes, 0, 0)
+
+
+def copies_kernel(count, block_ref, out_ref):
+    turned = block_ref[...].T
+    for i in range(count):
+        out_ref[i] = turned
+
+
+def copies_turned(block, count):
+    rows, cols = block.shape
+    return pl.pallas_call(
+        functools.partial(copies_kernel, count),
+        out_shape=jax.ShapeDtypeStruct((count, cols, rows), block.dtype),
+        in_specs=[pl.BlockSpec(memory_space=pltpu.VMEM)],
+        out_specs=pl.BlockSpec(memory_space=pltpu.VMEM),
+        cost_estimate=pl.CostEstimate(
+            flops=0, bytes_accessed=2 * (count + 1) * rows * cols, transcendentals=0
+        ),
+        compiler_params=pltpu.CompilerParams(vmem_limit_bytes=4 * 2**20),
+        name="copies_turned",
+    )(block)
 
 
 def swap_cores(block):
@@ -92,18 +113,18 @@
     rows, cols = weight_codes.shape
     tokens = kv_cotangent.shape[0]
 
-    cot = spread(kv_cotangent.T, GROUP, N_GROUP).reshape(-1, tokens)
-    input_other = swap_cores(layer_input)
+    cot = lax.all_to_all(copies_turned(kv_cotangent, N_GROUP), GROUP, 0, 0).reshape(-1, tokens)
     mine, order = collect(
         dequantize(weight_codes, block_scales), [(0, 0)], "xh", ((2, 0, 1), (1, 0, 1), (-1, 0, 1))
     )
-    cot, input_other, _ = lax.optimization_barrier((cot, input_other, mine))
+    cot, _ = lax.optimization_barrier((cot, mine))
     mine, order = collect(mine, order, "z", ((3, 0, 4), (-3, 0, 4)))
 
     halves = cot.reshape(N_CHIPS, 2, rows, tokens)
     keep = lax.dynamic_index_in_dim(halves, core, 1, keepdims=False)
     give = lax.dynamic_index_in_dim(halves, 1 - core, 1, keepdims=False)
     cot_other = swap_cores(give)
+    input_other = swap_cores(layer_input)
     pair = jnp.einsum("crt,td->crd", keep, layer_input, preferred_element_type=jnp.float32)
     pair += jnp.einsum("crt,td->crd", cot_other, input_other, preferred_element_type=jnp.float32)
     pieces = lax.all_to_all(pair.astype(jnp.bfloat16), CHIPS, 0, 0)
@@ -114,7 +135,6 @@
     squares = sum(squares[:, i : i + 128] for i in range(0, cols, 128))
     squares = spread(squares, CHIPS, N_CHIPS)
     mine, order = collect(mine, order, "z", ((1, 0, 12), (-1, 0, 8)))
-    squares, mine = lax.optimization_barrier((squares, mine))
     squares = spread(jnp.sum(squares, axis=0), ("core",) + GROUP, 2 * N_GROUP)
     weight = order_rows(mine, swap_cores(mine), order, rows)
     grad_input = jnp.einsum(

time: 154 us -> 163 us (1.058)
  waiting for transfers between devices: 54 us -> 66.7 us
  starting transfers between devices: 87.3 us -> 84.1 us
    all_to_all x3 -> x2, starting transfers between devices: 27 us -> 16 us  [spread(): lax.all_to_all(jnp.broadcast_to(block[None], (count, *block.shape)), axes...]
    all_to_all x0 -> x1, starting transfers between devices: none -> 9.26 us  [work(): lax.all_to_all(copies_turned(kv_cotangent, N_GROUP), GROUP, 0, 0)]
    ppermute x3, starting transfers between devices: 18.4 us -> 11 us  [swap_cores(): return lax.ppermute(block, 'core', [(0, 1), (1, 0)])]
    ppermute x7, waiting for transfers between devices: 36.4 us -> 43.7 us  [fetch(): lax.ppermute(block, axis, [(i, (i - distance) % size) for i in range(size)])]
    all_to_all x0 -> x1, waiting for transfers between devices: none -> 4.88 us  [work(): lax.all_to_all(copies_turned(kv_cotangent, N_GROUP), GROUP, 0, 0)]
    ppermute x7, starting transfers between devices: 22.9 us -> 27.2 us  [fetch(): lax.ppermute(block, axis, [(i, (i - distance) % size) for i in range(size)])]
    all_to_all x1, starting transfers between devices: 19 us -> 20.7 us  [work(): pieces = lax.all_to_all(pair.astype(jnp.bfloat16), CHIPS, 0, 0)]
    all_to_all x3 -> x2, waiting for transfers between devices: 16.6 us -> 17 us  [spread(): lax.all_to_all(jnp.broadcast_to(block[None], (count, *block.shape)), axes...]
  transfers between devices with their start and end apart: 14 -> 14, of which waited for: 5 -> 8; matrix products, arithmetic and copies ran while one was open for 3% -> 2% of each run, Pallas kernels for 0% -> 0%
where the time goes in v7:
time: 163 us; the launch traced here: 162 us
  starting transfers between devices  84.1 us (52%)
  waiting for transfers between devices  66.7 us (41%)
  matrix products  3.28 us (2%)
  local copies, waits for them, and re-layouts  2.93 us (2%)
  Pallas kernels  1.81 us (1%)
  other arithmetic  1.73 us (1%)
  between operations  1.66 us (1%)
    ppermute x7, waiting for transfers between devices, fetch(): lax.ppermute(block, axis, [(i, (i - distance) % size) for i in range(size)])  43.7 us
    ppermute x7, starting transfers between devices, fetch(): lax.ppermute(block, axis, [(i, (i - distance) % size) for i in range(size)])  27.2 us
    all_to_all x1, starting transfers between devices, work(): pieces = lax.all_to_all(pair.astype(jnp.bfloat16), CHIPS, 0, 0)  20.7 us
    all_to_all x2, waiting for transfers between devices, spread(): lax.all_to_all(jnp.broadcast_to(block[None], (count, *block.shape)), axes...  17 us
    all_to_all x2, starting transfers between devices, spread(): lax.all_to_all(jnp.broadcast_to(block[None], (count, *block.shape)), axes...  16 us
    ppermute x3, starting transfers between devices, swap_cores(): return lax.ppermute(block, 'core', [(0, 1), (1, 0)])  11 us
    all_to_all x1, starting transfers between devices, work(): lax.all_to_all(copies_turned(kv_cotangent, N_GROUP), GROUP, 0, 0)  9.26 us
    all_to_all x1, waiting for transfers between devices, work(): lax.all_to_all(copies_turned(kv_cotangent, N_GROUP), GROUP, 0, 0)  4.88 us
  transfers between devices with their start and end apart: 14, of which 8 were waited for; matrix products, arithmetic and copies ran while one was open for 2% of the time, Pallas kernels for 0%

profile of v7, /device:TPU:1, one launch (start us, length us, event | category | flops | bytes accessed | tf_op | source)
XLA Modules:
  0.0 162.3 jit_solution(2399786643669643139)
XLA Ops:
  0.6 0.8 copy-done
  1.5 1.1 copies_turned.1
  2.6 9.3 %all-to-all-start = ((bf16[16,128,256]{2,1,0:T(8,128)(2,1)}), bf16[16,128,256]{2,1,0:T(8,128)(2,1)S(1)}, u32[]{:S(2)}, u32[]{:S(2)}) async-start(bf16[16,128,256]{2,1,0:T(8,128)(2,1)} %copies_turned.1), calls=%async_computation | async-start | bytes 2097152 | tf_op jit(solution)/shard_map/all_to_all | solution.py:116
  12.1 4.0 %collective-permute-start.2 = (bf16[32,512]{1,0:T(8,128)(2,1)S(1)}, bf16[32,512]{1,0:T(8,128)(2,1)S(1)}, u32[]{:S(2)}, u32[]{:S(2)}) collective-permute-start(bf16[32,512]{1,0:T(8,128)(2,1)S(1)} %multiply_convert_fusion), channel_id=1, source_target_pairs={{0,256},{256,512},{512,768},{768,0},{1,257},{257,513},{513,769},{7... | collective-permute-start | bytes 98312 | tf_op jit(solution)/shard_map/ppermute | solution.py:71
  16.1 3.3 %collective-permute-start.1 = (bf16[32,512]{1,0:T(8,128)(2,1)S(1)}, bf16[32,512]{1,0:T(8,128)(2,1)S(1)}, u32[]{:S(2)}, u32[]{:S(2)}) collective-permute-start(bf16[32,512]{1,0:T(8,128)(2,1)S(1)} %multiply_convert_fusion), channel_id=1, source_target_pairs={{0,768},{256,0},{512,256},{768,512},{1,769},{257,1},{513,257},{769... | collective-permute-start | bytes 98312 | tf_op jit(solution)/shard_map/ppermute | solution.py:71
  19.5 6.2 %collective-permute-start = (bf16[32,512]{1,0:T(8,128)(2,1)S(1)}, bf16[32,512]{1,0:T(8,128)(2,1)S(1)}, u32[]{:S(2)}, u32[]{:S(2)}) collective-permute-start(bf16[32,512]{1,0:T(8,128)(2,1)S(1)} %multiply_convert_fusion), channel_id=1, source_target_pairs={{0,512},{256,768},{512,0},{768,256},{1,513},{257,769},{513,1},{769... | collective-permute-start | bytes 98312 | tf_op jit(solution)/shard_map/ppermute | solution.py:71
  25.7 2.3 %collective-permute-done.2 = bf16[32,512]{1,0:T(8,128)(2,1)S(1)} collective-permute-done((bf16[32,512]{1,0:T(8,128)(2,1)S(1)}, bf16[32,512]{1,0:T(8,128)(2,1)S(1)}, u32[]{:S(2)}, u32[]{:S(2)}) %collective-permute-start.2) | collective-permute-done | bytes 32800 | tf_op jit(solution)/shard_map/ppermute | solution.py:71
  28.0 2.4 %collective-permute-done = bf16[32,512]{1,0:T(8,128)(2,1)S(1)} collective-permute-done((bf16[32,512]{1,0:T(8,128)(2,1)S(1)}, bf16[32,512]{1,0:T(8,128)(2,1)S(1)}, u32[]{:S(2)}, u32[]{:S(2)}) %collective-permute-start) | collective-permute-done | bytes 32800 | tf_op jit(solution)/shard_map/ppermute | solution.py:71
  30.4 4.9 %all-to-all-done = bf16[16,128,256]{2,1,0:T(8,128)(2,1)S(1)} async-done(((bf16[16,128,256]{2,1,0:T(8,128)(2,1)}), bf16[16,128,256]{2,1,0:T(8,128)(2,1)S(1)}, u32[]{:S(2)}, u32[]{:S(2)}) %all-to-all-start) | async-done | bytes 1048608 | tf_op jit(solution)/shard_map/all_to_all | solution.py:116
  35.4 5.2 %collective-permute-start.3 = (bf16[32,32,256]{2,1,0:T(8,128)(2,1)S(1)}, bf16[32,32,256]{2,1,0:T(8,128)(2,1)S(1)}, u32[]{:S(2)}, u32[]{:S(2)}) collective-permute-start(bf16[32,32,256]{2,1,0:T(8,128)(2,1)S(1)} %dynamic-slice_bitcast_fusion), channel_id=1, source_target_pairs={{0,16},{16,0},{1,17},{17,1},{2,18},{18,2},{3,19},{19,3},{4,20},{20... | collective-permute-start | bytes 1572872 | tf_op jit(solution)/shard_map/ppermute | solution.py:66
  40.6 1.9 %collective-permute-start.4 = (bf16[256,512]{1,0:T(8,128)(2,1)S(1)}, bf16[256,512]{1,0:T(8,128)(2,1)S(1)}, u32[]{:S(2)}, u32[]{:S(2)}) collective-permute-start(bf16[256,512]{1,0:T(8,128)(2,1)S(1)} %copy-done.3), channel_id=1, source_target_pairs={{0,16},{16,0},{1,17},{17,1},{2,18},{18,2},{3,19},{19,3},{4,20},{20... | collective-permute-start | bytes 786440 | tf_op jit(solution)/shard_map/ppermute | solution.py:66
  42.9 1.1 collective-permute-done.4
  44.0 1.4 add_convert_fusion
  45.4 20.7 %all-to-all-start.1 = ((bf16[32,32,512]{2,1,0:T(8,128)(2,1)}), bf16[32,32,512]{2,1,0:T(8,128)(2,1)S(1)}, u32[]{:S(2)}, u32[]{:S(2)}) async-start(bf16[32,32,512]{2,1,0:T(8,128)(2,1)} %add_convert_fusion), calls=%async_computation.1 | async-start | bytes 2097152 | tf_op jit(solution)/shard_map/all_to_all | solution.py:130
  66.2 4.9 %collective-permute-start.6 = (bf16[128,512]{1,0:T(8,128)(2,1)S(1)}, bf16[128,512]{1,0:T(8,128)(2,1)S(1)}, u32[]{:S(2)}, u32[]{:S(2)}) collective-permute-start(bf16[128,512]{1,0:T(8,128)(2,1)S(1)} %pad_maximum_fusion.2), channel_id=1, source_target_pairs={{0,96},{32,128},{64,160},{96,192},{128,224},{160,0},{192,32},{224,... | collective-permute-start | bytes 393224 | tf_op jit(solution)/shard_map/ppermute | solution.py:71
  71.1 3.4 %collective-permute-start.5 = (bf16[128,512]{1,0:T(8,128)(2,1)S(1)}, bf16[128,512]{1,0:T(8,128)(2,1)S(1)}, u32[]{:S(2)}, u32[]{:S(2)}) collective-permute-start(bf16[128,512]{1,0:T(8,128)(2,1)S(1)} %pad_maximum_fusion.2), channel_id=1, source_target_pairs={{0,160},{32,192},{64,224},{96,0},{128,32},{160,64},{192,96},{224,1... | collective-permute-start | bytes 393224 | tf_op jit(solution)/shard_map/ppermute | solution.py:71
  74.5 32.5 %collective-permute-done.6 = bf16[128,512]{1,0:T(8,128)(2,1)S(1)} collective-permute-done((bf16[128,512]{1,0:T(8,128)(2,1)S(1)}, bf16[128,512]{1,0:T(8,128)(2,1)S(1)}, u32[]{:S(2)}, u32[]{:S(2)}) %collective-permute-start.6) | collective-permute-done | bytes 131104 | tf_op jit(solution)/shard_map/ppermute | solution.py:71
  107.0 1.9 %collective-permute-start.7 = (bf16[384,512]{1,0:T(8,128)(2,1)S(1)}, bf16[384,512]{1,0:T(8,128)(2,1)S(1)}, u32[]{:S(2)}, u32[]{:S(2)}) collective-permute-start(bf16[384,512]{1,0:T(8,128)(2,1)S(1)} %pad_maximum_fusion.1), channel_id=1, source_target_pairs={{0,224},{32,0},{64,32},{96,64},{128,96},{160,128},{192,160},{224,1... | collective-permute-start | bytes 1179656 | tf_op jit(solution)/shard_map/ppermute | solution.py:71
  109.0 3.4 %collective-permute-start.8 = (bf16[256,512]{1,0:T(8,128)(2,1)S(1)}, bf16[256,512]{1,0:T(8,128)(2,1)S(1)}, u32[]{:S(2)}, u32[]{:S(2)}) collective-permute-start(bf16[256,512]{1,0:T(8,128)(2,1)S(1)} %slice.19), channel_id=1, source_target_pairs={{0,32},{32,64},{64,96},{96,128},{128,160},{160,192},{192,224},{224... | collective-permute-start | bytes 786440 | tf_op jit(solution)/shard_map/ppermute | solution.py:71
  112.4 6.5 %collective-permute-done.8 = bf16[256,512]{1,0:T(8,128)(2,1)S(1)} collective-permute-done((bf16[256,512]{1,0:T(8,128)(2,1)S(1)}, bf16[256,512]{1,0:T(8,128)(2,1)S(1)}, u32[]{:S(2)}, u32[]{:S(2)}) %collective-permute-start.8) | collective-permute-done | bytes 262176 | tf_op jit(solution)/shard_map/ppermute | solution.py:71
  118.9 3.9 %collective-permute-start.9 = (bf16[1024,512]{1,0:T(8,128)(2,1)S(1)}, bf16[1024,512]{1,0:T(8,128)(2,1)S(1)}, u32[]{:S(2)}, u32[]{:S(2)}) collective-permute-start(bf16[1024,512]{1,0:T(8,128)(2,1)S(1)} %pad_maximum_fusion.mine_ref), channel_id=1, source_target_pairs={{0,16},{16,0},{1,17},{17,1},{2,18},{18,2},{3,19},{19,3},{4,20},{20... | collective-permute-start | bytes 3145736 | tf_op jit(solution)/shard_map/ppermute | solution.py:66
  123.0 0.7 broadcast_in_dim.4
  123.7 7.0 %all-to-all-start.2 = ((f32[32,8,128]{2,1,0:T(8,128)}), f32[32,8,128]{2,1,0:T(8,128)S(1)}, u32[]{:S(2)}, u32[]{:S(2)}) async-start(f32[32,8,128]{2,1,0:T(8,128)} %broadcast_in_dim.4), calls=%async_computation.2 | async-start | bytes 262144 | tf_op jit(solution)/shard_map/all_to_all | solution.py:41
  130.7 11.4 %all-to-all-done.2 = f32[32,8,128]{2,1,0:T(8,128)S(1)} async-done(((f32[32,8,128]{2,1,0:T(8,128)}), f32[32,8,128]{2,1,0:T(8,128)S(1)}, u32[]{:S(2)}, u32[]{:S(2)}) %all-to-all-start.2) | async-done | bytes 131104 | tf_op jit(solution)/shard_map/all_to_all | solution.py:41
  142.1 0.7 broadcast_in_dim.5
  142.8 9.0 %all-to-all-start.3 = ((f32[32,8,128]{2,1,0:T(8,128)}), f32[32,8,128]{2,1,0:T(8,128)S(1)}, u32[]{:S(2)}, u32[]{:S(2)}) async-start(f32[32,8,128]{2,1,0:T(8,128)} %broadcast_in_dim.5), calls=%async_computation.3 | async-start | bytes 262144 | tf_op jit(solution)/shard_map/all_to_all | solution.py:41
  151.9 0.7 order_rows.1
  152.6 0.5 copy-done.2
  153.1 1.4 convolution_convert_fusion
  154.5 5.7 %all-to-all-done.3 = f32[32,8,128]{2,1,0:T(8,128)S(1)} async-done(((f32[32,8,128]{2,1,0:T(8,128)}), f32[32,8,128]{2,1,0:T(8,128)S(1)}, u32[]{:S(2)}, u32[]{:S(2)}) %all-to-all-start.3) | async-done | bytes 131104 | tf_op jit(solution)/shard_map/all_to_all | solution.py:41
  160.2 0.6 reduce_sum.39
  161.6 0.7 multiply_subtract_fusion
  (37 shorter events, 1.1 us)
Async XLA Ops:
  0.6 0.8 copy-start
  1.5 10.4 %copy-start.8 = (bf16[32,2]{0,1:T(2,128)(2,1)S(1)}, bf16[32,2]{0,1:T(2,128)(2,1)}, u32[]{:S(2)}) copy-start(bf16[32,2]{0,1:T(2,128)(2,1)} %param.10) | copy-start | bytes 388
  1.5 10.6 %copy-start.7 = (bf16[32,512]{1,0:T(8,128)(2,1)S(1)}, bf16[32,512]{1,0:T(8,128)(2,1)}, u32[]{:S(2)}) copy-start(bf16[32,512]{1,0:T(8,128)(2,1)} %param.9) | copy-start | bytes 98308
  2.6 38.0 %copy-start.3 = (bf16[256,512]{1,0:T(8,128)(2,1)S(1)}, bf16[256,512]{1,0:T(8,128)(2,1)}, u32[]{:S(2)}) copy-start(bf16[256,512]{1,0:T(8,128)(2,1)} %param.7) | copy-start | bytes 786436
  2.6 32.8 %all-to-all-start = ((bf16[16,128,256]{2,1,0:T(8,128)(2,1)}), bf16[16,128,256]{2,1,0:T(8,128)(2,1)S(1)}, u32[]{:S(2)}, u32[]{:S(2)}) async-start(bf16[16,128,256]{2,1,0:T(8,128)(2,1)} %copies_turned.1), calls=%async_computation | async-start | bytes 2097152 | tf_op jit(solution)/shard_map/all_to_all | solution.py:116
  12.1 15.9 %collective-permute-start.2 = (bf16[32,512]{1,0:T(8,128)(2,1)S(1)}, bf16[32,512]{1,0:T(8,128)(2,1)S(1)}, u32[]{:S(2)}, u32[]{:S(2)}) collective-permute-start(bf16[32,512]{1,0:T(8,128)(2,1)S(1)} %multiply_convert_fusion), channel_id=1, source_target_pairs={{0,256},{256,512},{512,768},{768,0},{1,257},{257,513},{513,769},{7... | collective-permute-start | bytes 98312 | tf_op jit(solution)/shard_map/ppermute | solution.py:71
  16.1 11.8 %collective-permute-start.1 = (bf16[32,512]{1,0:T(8,128)(2,1)S(1)}, bf16[32,512]{1,0:T(8,128)(2,1)S(1)}, u32[]{:S(2)}, u32[]{:S(2)}) collective-permute-start(bf16[32,512]{1,0:T(8,128)(2,1)S(1)} %multiply_convert_fusion), channel_id=1, source_target_pairs={{0,768},{256,0},{512,256},{768,512},{1,769},{257,1},{513,257},{769... | collective-permute-start | bytes 98312 | tf_op jit(solution)/shard_map/ppermute | solution.py:71
  19.5 10.9 %collective-permute-start = (bf16[32,512]{1,0:T(8,128)(2,1)S(1)}, bf16[32,512]{1,0:T(8,128)(2,1)S(1)}, u32[]{:S(2)}, u32[]{:S(2)}) collective-permute-start(bf16[32,512]{1,0:T(8,128)(2,1)S(1)} %multiply_convert_fusion), channel_id=1, source_target_pairs={{0,512},{256,768},{512,0},{768,256},{1,513},{257,769},{513,1},{769... | collective-permute-start | bytes 98312 | tf_op jit(solution)/shard_map/ppermute | solution.py:71
  35.3 10.1 %copy-start.1 = (bf16[16,128,256]{2,1,0:T(8,128)(2,1)}, bf16[16,128,256]{2,1,0:T(8,128)(2,1)S(1)}, u32[]{:S(2)}) copy-start(bf16[16,128,256]{2,1,0:T(8,128)(2,1)S(1)} %all-to-all-done) | copy-start | bytes 3145732
  35.4 8.6 %collective-permute-start.3 = (bf16[32,32,256]{2,1,0:T(8,128)(2,1)S(1)}, bf16[32,32,256]{2,1,0:T(8,128)(2,1)S(1)}, u32[]{:S(2)}, u32[]{:S(2)}) collective-permute-start(bf16[32,32,256]{2,1,0:T(8,128)(2,1)S(1)} %dynamic-slice_bitcast_fusion), channel_id=1, source_target_pairs={{0,16},{16,0},{1,17},{17,1},{2,18},{18,2},{3,19},{19,3},{4,20},{20... | collective-permute-start | bytes 1572872 | tf_op jit(solution)/shard_map/ppermute | solution.py:66
  40.6 3.4 %collective-permute-start.4 = (bf16[256,512]{1,0:T(8,128)(2,1)S(1)}, bf16[256,512]{1,0:T(8,128)(2,1)S(1)}, u32[]{:S(2)}, u32[]{:S(2)}) collective-permute-start(bf16[256,512]{1,0:T(8,128)(2,1)S(1)} %copy-done.3), channel_id=1, source_target_pairs={{0,16},{16,0},{1,17},{17,1},{2,18},{18,2},{3,19},{19,3},{4,20},{20... | collective-permute-start | bytes 786440 | tf_op jit(solution)/shard_map/ppermute | solution.py:66
  45.4 61.6 %all-to-all-start.1 = ((bf16[32,32,512]{2,1,0:T(8,128)(2,1)}), bf16[32,32,512]{2,1,0:T(8,128)(2,1)S(1)}, u32[]{:S(2)}, u32[]{:S(2)}) async-start(bf16[32,32,512]{2,1,0:T(8,128)(2,1)} %add_convert_fusion), calls=%async_computation.1 | async-start | bytes 2097152 | tf_op jit(solution)/shard_map/all_to_all | solution.py:130
  66.2 40.8 %collective-permute-start.6 = (bf16[128,512]{1,0:T(8,128)(2,1)S(1)}, bf16[128,512]{1,0:T(8,128)(2,1)S(1)}, u32[]{:S(2)}, u32[]{:S(2)}) collective-permute-start(bf16[128,512]{1,0:T(8,128)(2,1)S(1)} %pad_maximum_fusion.2), channel_id=1, source_target_pairs={{0,96},{32,128},{64,160},{96,192},{128,224},{160,0},{192,32},{224,... | collective-permute-start | bytes 393224 | tf_op jit(solution)/shard_map/ppermute | solution.py:71
  71.1 35.9 %collective-permute-start.5 = (bf16[128,512]{1,0:T(8,128)(2,1)S(1)}, bf16[128,512]{1,0:T(8,128)(2,1)S(1)}, u32[]{:S(2)}, u32[]{:S(2)}) collective-permute-start(bf16[128,512]{1,0:T(8,128)(2,1)S(1)} %pad_maximum_fusion.2), channel_id=1, source_target_pairs={{0,160},{32,192},{64,224},{96,0},{128,32},{160,64},{192,96},{224,1... | collective-permute-start | bytes 393224 | tf_op jit(solution)/shard_map/ppermute | solution.py:71
  107.0 11.8 %collective-permute-start.7 = (bf16[384,512]{1,0:T(8,128)(2,1)S(1)}, bf16[384,512]{1,0:T(8,128)(2,1)S(1)}, u32[]{:S(2)}, u32[]{:S(2)}) collective-permute-start(bf16[384,512]{1,0:T(8,128)(2,1)S(1)} %pad_maximum_fusion.1), channel_id=1, source_target_pairs={{0,224},{32,0},{64,32},{96,64},{128,96},{160,128},{192,160},{224,1... | collective-permute-start | bytes 1179656 | tf_op jit(solution)/shard_map/ppermute | solution.py:71
  109.0 9.9 %collective-permute-start.8 = (bf16[256,512]{1,0:T(8,128)(2,1)S(1)}, bf16[256,512]{1,0:T(8,128)(2,1)S(1)}, u32[]{:S(2)}, u32[]{:S(2)}) collective-permute-start(bf16[256,512]{1,0:T(8,128)(2,1)S(1)} %slice.19), channel_id=1, source_target_pairs={{0,32},{32,64},{64,96},{96,128},{128,160},{160,192},{192,224},{224... | collective-permute-start | bytes 786440 | tf_op jit(solution)/shard_map/ppermute | solution.py:71
  118.9 32.9 %collective-permute-start.9 = (bf16[1024,512]{1,0:T(8,128)(2,1)S(1)}, bf16[1024,512]{1,0:T(8,128)(2,1)S(1)}, u32[]{:S(2)}, u32[]{:S(2)}) collective-permute-start(bf16[1024,512]{1,0:T(8,128)(2,1)S(1)} %pad_maximum_fusion.mine_ref), channel_id=1, source_target_pairs={{0,16},{16,0},{1,17},{17,1},{2,18},{18,2},{3,19},{19,3},{4,20},{20... | collective-permute-start | bytes 3145736 | tf_op jit(solution)/shard_map/ppermute | solution.py:66
  123.7 18.4 %all-to-all-start.2 = ((f32[32,8,128]{2,1,0:T(8,128)}), f32[32,8,128]{2,1,0:T(8,128)S(1)}, u32[]{:S(2)}, u32[]{:S(2)}) async-start(f32[32,8,128]{2,1,0:T(8,128)} %broadcast_in_dim.4), calls=%async_computation.2 | async-start | bytes 262144 | tf_op jit(solution)/shard_map/all_to_all | solution.py:41
  142.8 17.4 %all-to-all-start.3 = ((f32[32,8,128]{2,1,0:T(8,128)}), f32[32,8,128]{2,1,0:T(8,128)S(1)}, u32[]{:S(2)}, u32[]{:S(2)}) async-start(f32[32,8,128]{2,1,0:T(8,128)} %broadcast_in_dim.5), calls=%async_computation.3 | async-start | bytes 262144 | tf_op jit(solution)/shard_map/all_to_all | solution.py:41
  151.9 1.2 copy-start.2
  153.1 8.5 %copy-start.4 = (f32[32,512]{1,0:T(8,128)S(1)}, f32[32,512]{1,0:T(8,128)}, u32[]{:S(2)}) copy-start(f32[32,512]{1,0:T(8,128)} %param.11) | copy-start | bytes 196612
  153.1 8.5 %copy-start.5 = (f32[32,512]{1,0:T(8,128)S(1)}, f32[32,512]{1,0:T(8,128)}, u32[]{:S(2)}) copy-start(f32[32,512]{1,0:T(8,128)} %param.12) | copy-start | bytes 196612
  153.1 8.5 %copy-start.6 = (f32[32,512]{1,0:T(8,128)S(1)}, f32[32,512]{1,0:T(8,128)}, u32[]{:S(2)}) copy-start(f32[32,512]{1,0:T(8,128)} %param.13) | copy-start | bytes 196612
